TPU v7x, 32 devices: a whole 2x2x4 slice. The times are simulated.
32 devices in a mesh: gx: 4 (over z), gy: 4 (over x, core), gz: 2 (over y).
Axes of the slice: x: 2, y: 2, z: 4, core: 2. Of those that a mesh axis runs over, the one named last changes fastest.
Arguments:
- dist: float32 [19, 8, 32, 512], P(None, 'gx', 'gy', 'gz'), may hold values from 0.01 to 0.1
- site_kinds: int32 [8, 32, 512], P('gx', 'gy', 'gz'), may hold values from 0 to 3
- relax: float32 [8, 32, 512], P('gx', 'gy', 'gz'), may hold values from 0.5 to 1.9
- inflow: float32 [3, 8, 32, 512], P(None, 'gx', 'gy', 'gz'), may hold values from -0.3 to 0.3
Outputs:
- density: float32 [8, 32, 512], P('gx', 'gy', 'gz')
- momentum: float32 [3, 8, 32, 512], P(None, 'gx', 'gy', 'gz')
All inputs are finite; a program needn't handle non-finite values.
Results may differ from a plain program's by a relative error of at most 0.0001.
Values sent between devices are 32-bit elements; how exact they have to be, the bound alone decides.
No kernel may reach another device: no remote copies, remote signals or barrier semaphores. Data moves between devices by JAX's collectives and lax.ppermute only.
A program may use at most 64 MiB of HBM per device.

v0:
```python
import jax
import jax.numpy as jnp
import numpy as np
from jax import lax
from jax.sharding import PartitionSpec as P

STEPS = 2


VELOCITIES = [
    (0, 0, 0),
    (1, 0, 0),
    (-1, 0, 0),
    (0, 1, 0),
    (0, -1, 0),
    (0, 0, 1),
    (0, 0, -1),
    (1, 1, 0),
    (-1, -1, 0),
    (1, -1, 0),
    (-1, 1, 0),
    (1, 0, 1),
    (-1, 0, -1),
    (1, 0, -1),
    (-1, 0, 1),
    (0, 1, 1),
    (0, -1, -1),
    (0, 1, -1),
    (0, -1, 1),
]
WEIGHTS = [1.0 / 3.0] + [1.0 / 18.0] * 6 + [1.0 / 36.0] * 12
OPPOSITE = [0, 2, 1, 4, 3, 6, 5, 8, 7, 10, 9, 12, 11, 14, 13, 16, 15, 18, 17]


def passed_along(block, axis, distance):
    devices = range(lax.axis_size(axis))
    route = [(i - distance, i) for i in devices if i - distance in devices]
    return lax.ppermute(block, axis, route)


def moments(dist):
    table = np.array(VELOCITIES, dtype=np.float32)
    density = jnp.sum(dist, axis=0)
    parts = []
    for axis_id in range(3):
        column = jnp.asarray(table[:, axis_id]).astype(dist.dtype)
        parts.append(jnp.sum(column[:, None, None, None] * dist, axis=0))
    return (density, jnp.stack(parts))


def equilibrium(density, speed):
    usq = speed[0] * speed[0] + speed[1] * speed[1] + speed[2] * speed[2]
    result = []
    for index in range(19):
        vel = VELOCITIES[index]
        along = vel[0] * speed[0] + vel[1] * speed[1] + vel[2] * speed[2]
        result.append(WEIGHTS[index] * (density + 3.0 * along + 4.5 * along * along - 1.5 * usq))
    return jnp.stack(result)


def collide(dist, site_kinds, relax, inflow):
    density, speed = moments(dist)
    fluid = dist - relax[None] * (dist - equilibrium(density, speed))
    wall = dist[np.array(OPPOSITE)]
    inlet = equilibrium(density, inflow)
    outlet = equilibrium(jnp.ones_like(density), speed)
    kinds = site_kinds[None]
    return jnp.where(
        kinds == 0, wall, jnp.where(kinds == 1, fluid, jnp.where(kinds == 2, inlet, outlet))
    )


def chosen(axis_id, sign):
    return [index for index in range(19) if VELOCITIES[index][axis_id] == sign]


def forward(stack, edge, dim):
    inner = lax.slice_in_dim(stack, 0, stack.shape[dim] - 1, axis=dim)
    return jnp.concatenate([jnp.expand_dims(edge, dim), inner], axis=dim)


def backward(stack, edge, dim):
    inner = lax.slice_in_dim(stack, 1, stack.shape[dim], axis=dim)
    return jnp.concatenate([inner, jnp.expand_dims(edge, dim)], axis=dim)


def last_plane(stack, dim):
    return lax.index_in_dim(stack, stack.shape[dim] - 1, axis=dim, keepdims=False)


def first_plane(stack, dim):
    return lax.index_in_dim(stack, 0, axis=dim, keepdims=False)


def shards(dist, site_kinds, relax, inflow):
    field = dist
    for step in range(STEPS):
        post = collide(field, site_kinds, relax, inflow)
        pops = [post[index] for index in range(19)]
        upper = chosen(0, 1)
        lower = chosen(0, -1)
        stack_up = jnp.stack([pops[index] for index in upper])
        stack_down = jnp.stack([pops[index] for index in lower])
        edge_up = passed_along(last_plane(stack_up, 1), "gx", 1)
        edge_down = passed_along(first_plane(stack_down, 1), "gx", -1)
        stack_up = forward(stack_up, edge_up, 1)
        stack_down = backward(stack_down, edge_down, 1)
        for slot, index in enumerate(upper):
            pops[index] = stack_up[slot]
        for slot, index in enumerate(lower):
            pops[index] = stack_down[slot]
        upper = chosen(1, 1)
        lower = chosen(1, -1)
        stack_up = jnp.stack([pops[index] for index in upper])
        stack_down = jnp.stack([pops[index] for index in lower])
        edge_up = passed_along(last_plane(stack_up, 2), "gy", 1)
        edge_down = passed_along(first_plane(stack_down, 2), "gy", -1)
        stack_up = forward(stack_up, edge_up, 2)
        stack_down = backward(stack_down, edge_down, 2)
        for slot, index in enumerate(upper):
            pops[index] = stack_up[slot]
        for slot, index in enumerate(lower):
            pops[index] = stack_down[slot]
        upper = chosen(2, 1)
        lower = chosen(2, -1)
        stack_up = jnp.stack([pops[index] for index in upper])
        stack_down = jnp.stack([pops[index] for index in lower])
        edge_up = passed_along(last_plane(stack_up, 3), "gz", 1)
        edge_down = passed_along(first_plane(stack_down, 3), "gz", -1)
        stack_up = forward(stack_up, edge_up, 3)
        stack_down = backward(stack_down, edge_down, 3)
        for slot, index in enumerate(upper):
            pops[index] = stack_up[slot]
        for slot, index in enumerate(lower):
            pops[index] = stack_down[slot]
        field = jnp.stack(pops)
    return moments(field)


def solution(mesh):
    return jax.shard_map(
        shards,
        mesh=mesh,
        in_specs=(
            P(None, "gx", "gy", "gz"),
            P("gx", "gy", "gz"),
            P("gx", "gy", "gz"),
            P(None, "gx", "gy", "gz"),
        ),
        out_specs=(P("gx", "gy", "gz"), P(None, "gx", "gy", "gz")),
        check_vma=False,
    )
```

profile of v0, /device:TPU:10, one launch (start us, length us, event | category | flops | bytes accessed | tf_op | source)
XLA Modules:
  0.0 61.5 jit_solution(11848728566785142180)
XLA Ops:
  0.6 0.0 copy-start.4
  0.6 0.0 copy-start.5
  0.7 0.0 copy-start.6
  0.7 0.6 %copy-done.4 = f32[19]{0:T(128)S(1)} copy-done((f32[19]{0:T(128)S(1)}, f32[19]{0:T(128)}, u32[]{:S(2)}) %copy-start.4) | copy-done | bytes 100
  1.3 0.0 copy-done.5
  1.3 0.0 copy-done.6
  1.3 1.1 %multiply_reduce_fusion.8 = (f32[2,8,256]{2,1,0:T(8,128)S(1)}, f32[2,8,256]{2,1,0:T(8,128)S(1)}, f32[2,8,256]{2,1,0:T(8,128)S(1)}, f32[2,8,256]{2,1,0:T(8,128)S(1)}) fusion(f32[19,2,8,256]{3,2,1,0:T(8,128)} %param.17, f32[19]{0:T(128)S(1)} %copy-done.4, f32[19]{0:T(128)S(1)} %copy-done.5, f32[19]{0:T(128)S(1)} %copy-done.6), kind=kLoop, calls=%fused_computation.216 | loop fusion | flops 528384 | bytes 377060 | tf_op jit(solution)/shard_map/reduce_sum | solution.py:47
  2.9 0.0 copy-start
  2.9 0.8 %copy-done = f32[3,2,8,256]{3,2,1,0:T(8,128)S(1)} copy-done((f32[3,2,8,256]{3,2,1,0:T(8,128)S(1)}, f32[3,2,8,256]{3,2,1,0:T(8,128)}, u32[]{:S(2)}) %copy-start) | copy-done | bytes 49176
  4.0 0.0 copy-start.1
  4.1 0.0 copy-start.3
  4.1 0.7 %copy-done.3 = s32[2,8,256]{2,1,0:T(8,128)S(1)} copy-done((s32[2,8,256]{2,1,0:T(8,128)S(1)}, s32[2,8,256]{2,1,0:T(8,128)}, u32[]{:S(2)}) %copy-start.3) | copy-done | bytes 16408
  4.8 0.6 %copy-done.7 = s32[19]{0:T(128)S(1)} copy-done((s32[19]{0:T(128)S(1)}, s32[19]{0:T(128)}, u32[]{:S(2)}) %copy-start.7) | copy-done | bytes 100
  5.5 0.6 gather_fusion
  6.1 0.1 copy-done.2
  6.2 0.2 select_select_fusion.1
  6.5 3.5 %collective-permute-start = (f32[5,8,256]{2,1,0:T(8,128)S(1)}, f32[5,8,256]{2,1,0:T(8,128)S(1)}, u32[]{:S(2)}, u32[]{:S(2)}) collective-permute-start(f32[5,8,256]{2,1,0:T(8,128)S(1)} %get-tuple-element.132), channel_id=1, source_target_pairs={{0,8},{8,16},{16,24},{1,9},{9,17},{17,25},{2,10},{10,18},{18,26},{... | collective-permute-start | bytes 122888 | tf_op jit(solution)/shard_map/ppermute | solution.py:38
  10.0 2.4 %collective-permute-start.1 = (f32[5,8,256]{2,1,0:T(8,128)S(1)}, f32[5,8,256]{2,1,0:T(8,128)S(1)}, u32[]{:S(2)}, u32[]{:S(2)}) collective-permute-start(f32[5,8,256]{2,1,0:T(8,128)S(1)} %get-tuple-element.131), channel_id=1, source_target_pairs={{8,0},{16,8},{24,16},{9,1},{17,9},{25,17},{10,2},{18,10},{26,18},{... | collective-permute-start | bytes 122888 | tf_op jit(solution)/shard_map/ppermute | solution.py:38
  12.4 3.5 %collective-permute-done.1 = f32[5,8,256]{2,1,0:T(8,128)S(1)} collective-permute-done((f32[5,8,256]{2,1,0:T(8,128)S(1)}, f32[5,8,256]{2,1,0:T(8,128)S(1)}, u32[]{:S(2)}, u32[]{:S(2)}) %collective-permute-start.1) | collective-permute-done | bytes 40992 | tf_op jit(solution)/shard_map/ppermute | solution.py:38
  16.0 1.9 %collective-permute-start.3 = (f32[5,2,256]{2,1,0:T(2,128)S(1)}, f32[5,2,256]{2,1,0:T(2,128)S(1)}, u32[]{:S(2)}, u32[]{:S(2)}) collective-permute-start(f32[5,2,256]{2,1,0:T(2,128)S(1)} %bitcast.931), channel_id=1, source_target_pairs={{2,0},{4,2},{6,4},{3,1},{5,3},{7,5},{10,8},{12,10},{14,12},{11,9},... | collective-permute-start | bytes 30728 | tf_op jit(solution)/shard_map/ppermute | solution.py:38
  18.0 2.4 %collective-permute-start.2 = (f32[5,2,256]{2,1,0:T(2,128)S(1)}, f32[5,2,256]{2,1,0:T(2,128)S(1)}, u32[]{:S(2)}, u32[]{:S(2)}) collective-permute-start(f32[5,2,256]{2,1,0:T(2,128)S(1)} %bitcast.935), channel_id=1, source_target_pairs={{0,2},{2,4},{4,6},{1,3},{3,5},{5,7},{8,10},{10,12},{12,14},{9,11},... | collective-permute-start | bytes 30728 | tf_op jit(solution)/shard_map/ppermute | solution.py:38
  20.4 2.5 %collective-permute-done.2 = f32[5,2,256]{2,1,0:T(2,128)S(1)} collective-permute-done((f32[5,2,256]{2,1,0:T(2,128)S(1)}, f32[5,2,256]{2,1,0:T(2,128)S(1)}, u32[]{:S(2)}, u32[]{:S(2)}) %collective-permute-start.2) | collective-permute-done | bytes 10272 | tf_op jit(solution)/shard_map/ppermute | solution.py:38
  23.0 0.1 slice_reduce_fusion.2
  23.1 1.3 %collective-permute-start.5 = (f32[5,2,8]{2,1,0:T(2,128)S(1)}, f32[5,2,8]{2,1,0:T(2,128)S(1)}, u32[]{:S(2)}, u32[]{:S(2)}) collective-permute-start(f32[5,2,8]{2,1,0:T(2,128)S(1)} %slice_reduce_fusion.2), channel_id=1, source_target_pairs={{1,0},{3,2},{5,4},{7,6},{9,8},{11,10},{13,12},{15,14},{17,16},{19,... | collective-permute-start | bytes 968 | tf_op jit(solution)/shard_map/ppermute | solution.py:38
  24.4 0.2 slice_reduce_fusion.3
  24.6 4.5 %collective-permute-start.4 = (f32[5,2,8]{2,1,0:T(2,128)S(1)}, f32[5,2,8]{2,1,0:T(2,128)S(1)}, u32[]{:S(2)}, u32[]{:S(2)}) collective-permute-start(f32[5,2,8]{2,1,0:T(2,128)S(1)} %slice_reduce_fusion.3), channel_id=1, source_target_pairs={{0,1},{2,3},{4,5},{6,7},{8,9},{10,11},{12,13},{14,15},{16,17},{18,... | collective-permute-start | bytes 968 | tf_op jit(solution)/shard_map/ppermute | solution.py:38
  29.2 0.1 slice.662
  29.3 0.1 copy.51
  29.4 1.1 %collective-permute-done.4 = f32[5,2,8]{2,1,0:T(2,128)S(1)} collective-permute-done((f32[5,2,8]{2,1,0:T(2,128)S(1)}, f32[5,2,8]{2,1,0:T(2,128)S(1)}, u32[]{:S(2)}, u32[]{:S(2)}) %collective-permute-start.4) | collective-permute-done | bytes 352 | tf_op jit(solution)/shard_map/ppermute | solution.py:38
  30.5 0.1 copy.50
  30.6 0.1 fusion.191
  30.7 0.1 constant_dynamic-update-slice_fusion.96
  30.8 0.1 constant_dynamic-update-slice_fusion.95
  30.9 0.1 fusion.182
  30.9 0.1 constant_dynamic-update-slice_fusion.91
  31.1 0.1 constant_dynamic-update-slice_fusion.87
  31.1 0.1 multiply_reduce_fusion.5
  31.3 0.6 gather_fusion.1
  32.5 0.2 select_select_fusion
  32.8 3.5 %collective-permute-start.6 = (f32[5,8,256]{2,1,0:T(8,128)S(1)}, f32[5,8,256]{2,1,0:T(8,128)S(1)}, u32[]{:S(2)}, u32[]{:S(2)}) collective-permute-start(f32[5,8,256]{2,1,0:T(8,128)S(1)} %get-tuple-element.120), channel_id=1, source_target_pairs={{0,8},{8,16},{16,24},{1,9},{9,17},{17,25},{2,10},{10,18},{18,26},{... | collective-permute-start | bytes 122888 | tf_op jit(solution)/shard_map/ppermute | solution.py:38
  36.3 2.4 %collective-permute-start.7 = (f32[5,8,256]{2,1,0:T(8,128)S(1)}, f32[5,8,256]{2,1,0:T(8,128)S(1)}, u32[]{:S(2)}, u32[]{:S(2)}) collective-permute-start(f32[5,8,256]{2,1,0:T(8,128)S(1)} %get-tuple-element.119), channel_id=1, source_target_pairs={{8,0},{16,8},{24,16},{9,1},{17,9},{25,17},{10,2},{18,10},{26,18},{... | collective-permute-start | bytes 122888 | tf_op jit(solution)/shard_map/ppermute | solution.py:38
  38.7 0.0 collective-permute-done.6
  38.7 3.5 %collective-permute-done.7 = f32[5,8,256]{2,1,0:T(8,128)S(1)} collective-permute-done((f32[5,8,256]{2,1,0:T(8,128)S(1)}, f32[5,8,256]{2,1,0:T(8,128)S(1)}, u32[]{:S(2)}, u32[]{:S(2)}) %collective-permute-start.7) | collective-permute-done | bytes 40992 | tf_op jit(solution)/shard_map/ppermute | solution.py:38
  42.3 1.9 %collective-permute-start.9 = (f32[5,2,256]{2,1,0:T(2,128)S(1)}, f32[5,2,256]{2,1,0:T(2,128)S(1)}, u32[]{:S(2)}, u32[]{:S(2)}) collective-permute-start(f32[5,2,256]{2,1,0:T(2,128)S(1)} %bitcast.933), channel_id=1, source_target_pairs={{2,0},{4,2},{6,4},{3,1},{5,3},{7,5},{10,8},{12,10},{14,12},{11,9},... | collective-permute-start | bytes 30728 | tf_op jit(solution)/shard_map/ppermute | solution.py:38
  44.3 2.4 %collective-permute-start.8 = (f32[5,2,256]{2,1,0:T(2,128)S(1)}, f32[5,2,256]{2,1,0:T(2,128)S(1)}, u32[]{:S(2)}, u32[]{:S(2)}) collective-permute-start(f32[5,2,256]{2,1,0:T(2,128)S(1)} %bitcast.937), channel_id=1, source_target_pairs={{0,2},{2,4},{4,6},{1,3},{3,5},{5,7},{8,10},{10,12},{12,14},{9,11},... | collective-permute-start | bytes 30728 | tf_op jit(solution)/shard_map/ppermute | solution.py:38
  46.8 2.5 %collective-permute-done.8 = f32[5,2,256]{2,1,0:T(2,128)S(1)} collective-permute-done((f32[5,2,256]{2,1,0:T(2,128)S(1)}, f32[5,2,256]{2,1,0:T(2,128)S(1)}, u32[]{:S(2)}, u32[]{:S(2)}) %collective-permute-start.8) | collective-permute-done | bytes 10272 | tf_op jit(solution)/shard_map/ppermute | solution.py:38
  49.4 0.2 slice_reduce_fusion.1
  49.5 4.2 %collective-permute-start.10 = (f32[5,2,8]{2,1,0:T(2,128)S(1)}, f32[5,2,8]{2,1,0:T(2,128)S(1)}, u32[]{:S(2)}, u32[]{:S(2)}) collective-permute-start(f32[5,2,8]{2,1,0:T(2,128)S(1)} %slice_reduce_fusion.1), channel_id=1, source_target_pairs={{0,1},{2,3},{4,5},{6,7},{8,9},{10,11},{12,13},{14,15},{16,17},{18,... | collective-permute-start | bytes 968 | tf_op jit(solution)/shard_map/ppermute | solution.py:38
  53.7 0.1 slice_reduce_fusion
  53.8 1.3 %collective-permute-start.11 = (f32[5,2,8]{2,1,0:T(2,128)S(1)}, f32[5,2,8]{2,1,0:T(2,128)S(1)}, u32[]{:S(2)}, u32[]{:S(2)}) collective-permute-start(f32[5,2,8]{2,1,0:T(2,128)S(1)} %slice_reduce_fusion), channel_id=1, source_target_pairs={{1,0},{3,2},{5,4},{7,6},{9,8},{11,10},{13,12},{15,14},{17,16},{19,... | collective-permute-start | bytes 968 | tf_op jit(solution)/shard_map/ppermute | solution.py:38
  55.1 0.1 slice.717
  55.2 0.1 copy.61
  55.3 4.0 %collective-permute-done.11 = f32[5,2,8]{2,1,0:T(2,128)S(1)} collective-permute-done((f32[5,2,8]{2,1,0:T(2,128)S(1)}, f32[5,2,8]{2,1,0:T(2,128)S(1)}, u32[]{:S(2)}, u32[]{:S(2)}) %collective-permute-start.11) | collective-permute-done | bytes 352 | tf_op jit(solution)/shard_map/ppermute | solution.py:38
  59.3 0.1 copy.62
  59.5 0.1 constant_dynamic-update-slice_fusion.198
  59.5 0.1 constant_dynamic-update-slice_fusion.197
  59.7 0.1 constant_dynamic-update-slice_fusion.193
  59.7 0.1 constant_dynamic-update-slice_fusion.192
  59.8 0.1 constant_dynamic-update-slice_fusion.191
  59.9 0.1 constant_dynamic-update-slice_fusion.190
  60.0 0.1 constant_dynamic-update-slice_fusion.189
  60.0 0.1 multiply_reduce_fusion.2
  60.2 0.6 %pad_maximum_fusion = f32[3,2,8,256]{3,2,1,0:T(8,128)} fusion(f32[1,2,8,256]{3,2,1,0:T(8,128)S(1)} %bitcast.929, f32[1,2,8,256]{3,2,1,0:T(8,128)S(1)} %bitcast.930, f32[1,2,8,256]{3,2,1,0:T(8,128)S(1)} %bitcast.928), kind=kLoop, calls=%fused_computation.265 | loop fusion | flops 24576 | bytes 98304 | tf_op jit(solution)/shard_map/stack | solution.py:48
  60.8 0.6 %bitcast_add_fusion = f32[2,8,256]{2,1,0:T(8,128)} fusion(f32[1,2,8,256]{3,2,1,0:T(8,128)S(1)} %get-tuple-element.13, f32[2,8,256]{2,1,0:T(8,128)S(1)} %reduce_sum.851, f32[2,8,256]{2,1,0:T(8,128)S(1)} %reduce_sum.849, f32[2,8,256]{2,1,0:T(8,128)S(1)} %reduce_sum.847, f32[1,2,8,256]{3,2,1,0:T(8,128)S(1)} %get-tuple-element.21, ...), kind=kLoop, calls=%fused_computation.391 | loop fusion | flops 73728 | bytes 442368 | tf_op jit(solution)/shard_map/reduce_sum | solution.py:43
  (146 shorter events, 1.7 us)
Async XLA Ops:
  0.6 0.7 %copy-start.4 = (f32[19]{0:T(128)S(1)}, f32[19]{0:T(128)}, u32[]{:S(2)}) copy-start(f32[19]{0:T(128)} %constant.17.clone) | copy-start | bytes 232
  0.6 0.7 %copy-start.5 = (f32[19]{0:T(128)S(1)}, f32[19]{0:T(128)}, u32[]{:S(2)}) copy-start(f32[19]{0:T(128)} %constant.38.clone) | copy-start | bytes 232
  0.7 0.7 %copy-start.6 = (f32[19]{0:T(128)S(1)}, f32[19]{0:T(128)}, u32[]{:S(2)}) copy-start(f32[19]{0:T(128)} %constant.39.clone) | copy-start | bytes 232
  2.9 0.8 %copy-start = (f32[3,2,8,256]{3,2,1,0:T(8,128)S(1)}, f32[3,2,8,256]{3,2,1,0:T(8,128)}, u32[]{:S(2)}) copy-start(f32[3,2,8,256]{3,2,1,0:T(8,128)} %param.20) | copy-start | bytes 147460
  4.0 1.5 %copy-start.1 = (f32[19,2,8,256]{3,2,1,0:T(8,128)S(1)}, f32[19,2,8,256]{3,2,1,0:T(8,128)}, u32[]{:S(2)}) copy-start(f32[19,2,8,256]{3,2,1,0:T(8,128)} %param.17) | copy-start | bytes 933892
  4.1 0.7 %copy-start.3 = (s32[2,8,256]{2,1,0:T(8,128)S(1)}, s32[2,8,256]{2,1,0:T(8,128)}, u32[]{:S(2)}) copy-start(s32[2,8,256]{2,1,0:T(8,128)} %param.18) | copy-start | bytes 49156
  4.8 0.7 %copy-start.7 = (s32[19]{0:T(128)S(1)}, s32[19]{0:T(128)}, u32[]{:S(2)}) copy-start(s32[19]{0:T(128)} %constant.47) | copy-start | bytes 232
  5.5 0.7 %copy-start.2 = (f32[2,8,256]{2,1,0:T(8,128)S(1)}, f32[2,8,256]{2,1,0:T(8,128)}, u32[]{:S(2)}) copy-start(f32[2,8,256]{2,1,0:T(8,128)} %param.19) | copy-start | bytes 49156
  6.5 5.9 %collective-permute-start = (f32[5,8,256]{2,1,0:T(8,128)S(1)}, f32[5,8,256]{2,1,0:T(8,128)S(1)}, u32[]{:S(2)}, u32[]{:S(2)}) collective-permute-start(f32[5,8,256]{2,1,0:T(8,128)S(1)} %get-tuple-element.132), channel_id=1, source_target_pairs={{0,8},{8,16},{16,24},{1,9},{9,17},{17,25},{2,10},{10,18},{18,26},{... | collective-permute-start | bytes 122888 | tf_op jit(solution)/shard_map/ppermute | solution.py:38
  10.0 5.9 %collective-permute-start.1 = (f32[5,8,256]{2,1,0:T(8,128)S(1)}, f32[5,8,256]{2,1,0:T(8,128)S(1)}, u32[]{:S(2)}, u32[]{:S(2)}) collective-permute-start(f32[5,8,256]{2,1,0:T(8,128)S(1)} %get-tuple-element.131), channel_id=1, source_target_pairs={{8,0},{16,8},{24,16},{9,1},{17,9},{25,17},{10,2},{18,10},{26,18},{... | collective-permute-start | bytes 122888 | tf_op jit(solution)/shard_map/ppermute | solution.py:38
  16.0 4.4 %collective-permute-start.3 = (f32[5,2,256]{2,1,0:T(2,128)S(1)}, f32[5,2,256]{2,1,0:T(2,128)S(1)}, u32[]{:S(2)}, u32[]{:S(2)}) collective-permute-start(f32[5,2,256]{2,1,0:T(2,128)S(1)} %bitcast.931), channel_id=1, source_target_pairs={{2,0},{4,2},{6,4},{3,1},{5,3},{7,5},{10,8},{12,10},{14,12},{11,9},... | collective-permute-start | bytes 30728 | tf_op jit(solution)/shard_map/ppermute | solution.py:38
  18.0 5.0 %collective-permute-start.2 = (f32[5,2,256]{2,1,0:T(2,128)S(1)}, f32[5,2,256]{2,1,0:T(2,128)S(1)}, u32[]{:S(2)}, u32[]{:S(2)}) collective-permute-start(f32[5,2,256]{2,1,0:T(2,128)S(1)} %bitcast.935), channel_id=1, source_target_pairs={{0,2},{2,4},{4,6},{1,3},{3,5},{5,7},{8,10},{10,12},{12,14},{9,11},... | collective-permute-start | bytes 30728 | tf_op jit(solution)/shard_map/ppermute | solution.py:38
  23.1 6.1 %collective-permute-start.5 = (f32[5,2,8]{2,1,0:T(2,128)S(1)}, f32[5,2,8]{2,1,0:T(2,128)S(1)}, u32[]{:S(2)}, u32[]{:S(2)}) collective-permute-start(f32[5,2,8]{2,1,0:T(2,128)S(1)} %slice_reduce_fusion.2), channel_id=1, source_target_pairs={{1,0},{3,2},{5,4},{7,6},{9,8},{11,10},{13,12},{15,14},{17,16},{19,... | collective-permute-start | bytes 968 | tf_op jit(solution)/shard_map/ppermute | solution.py:38
  24.6 5.9 %collective-permute-start.4 = (f32[5,2,8]{2,1,0:T(2,128)S(1)}, f32[5,2,8]{2,1,0:T(2,128)S(1)}, u32[]{:S(2)}, u32[]{:S(2)}) collective-permute-start(f32[5,2,8]{2,1,0:T(2,128)S(1)} %slice_reduce_fusion.3), channel_id=1, source_target_pairs={{0,1},{2,3},{4,5},{6,7},{8,9},{10,11},{12,13},{14,15},{16,17},{18,... | collective-permute-start | bytes 968 | tf_op jit(solution)/shard_map/ppermute | solution.py:38
  32.8 5.9 %collective-permute-start.6 = (f32[5,8,256]{2,1,0:T(8,128)S(1)}, f32[5,8,256]{2,1,0:T(8,128)S(1)}, u32[]{:S(2)}, u32[]{:S(2)}) collective-permute-start(f32[5,8,256]{2,1,0:T(8,128)S(1)} %get-tuple-element.120), channel_id=1, source_target_pairs={{0,8},{8,16},{16,24},{1,9},{9,17},{17,25},{2,10},{10,18},{18,26},{... | collective-permute-start | bytes 122888 | tf_op jit(solution)/shard_map/ppermute | solution.py:38
  36.3 5.9 %collective-permute-start.7 = (f32[5,8,256]{2,1,0:T(8,128)S(1)}, f32[5,8,256]{2,1,0:T(8,128)S(1)}, u32[]{:S(2)}, u32[]{:S(2)}) collective-permute-start(f32[5,8,256]{2,1,0:T(8,128)S(1)} %get-tuple-element.119), channel_id=1, source_target_pairs={{8,0},{16,8},{24,16},{9,1},{17,9},{25,17},{10,2},{18,10},{26,18},{... | collective-permute-start | bytes 122888 | tf_op jit(solution)/shard_map/ppermute | solution.py:38
  42.3 4.4 %collective-permute-start.9 = (f32[5,2,256]{2,1,0:T(2,128)S(1)}, f32[5,2,256]{2,1,0:T(2,128)S(1)}, u32[]{:S(2)}, u32[]{:S(2)}) collective-permute-start(f32[5,2,256]{2,1,0:T(2,128)S(1)} %bitcast.933), channel_id=1, source_target_pairs={{2,0},{4,2},{6,4},{3,1},{5,3},{7,5},{10,8},{12,10},{14,12},{11,9},... | collective-permute-start | bytes 30728 | tf_op jit(solution)/shard_map/ppermute | solution.py:38
  44.3 5.0 %collective-permute-start.8 = (f32[5,2,256]{2,1,0:T(2,128)S(1)}, f32[5,2,256]{2,1,0:T(2,128)S(1)}, u32[]{:S(2)}, u32[]{:S(2)}) collective-permute-start(f32[5,2,256]{2,1,0:T(2,128)S(1)} %bitcast.937), channel_id=1, source_target_pairs={{0,2},{2,4},{4,6},{1,3},{3,5},{5,7},{8,10},{10,12},{12,14},{9,11},... | collective-permute-start | bytes 30728 | tf_op jit(solution)/shard_map/ppermute | solution.py:38
  49.5 5.7 %collective-permute-start.10 = (f32[5,2,8]{2,1,0:T(2,128)S(1)}, f32[5,2,8]{2,1,0:T(2,128)S(1)}, u32[]{:S(2)}, u32[]{:S(2)}) collective-permute-start(f32[5,2,8]{2,1,0:T(2,128)S(1)} %slice_reduce_fusion.1), channel_id=1, source_target_pairs={{0,1},{2,3},{4,5},{6,7},{8,9},{10,11},{12,13},{14,15},{16,17},{18,... | collective-permute-start | bytes 968 | tf_op jit(solution)/shard_map/ppermute | solution.py:38
  53.8 5.5 %collective-permute-start.11 = (f32[5,2,8]{2,1,0:T(2,128)S(1)}, f32[5,2,8]{2,1,0:T(2,128)S(1)}, u32[]{:S(2)}, u32[]{:S(2)}) collective-permute-start(f32[5,2,8]{2,1,0:T(2,128)S(1)} %slice_reduce_fusion), channel_id=1, source_target_pairs={{1,0},{3,2},{5,4},{7,6},{9,8},{11,10},{13,12},{15,14},{17,16},{19,... | collective-permute-start | bytes 968 | tf_op jit(solution)/shard_map/ppermute | solution.py:38
where the time goes:
time: 62 us; the launch traced here: 61.5 us
  starting transfers between devices  31.6 us (51%)
  waiting for transfers between devices  17.2 us (28%)
  local copies, waits for them, and re-layouts  5.53 us (9%)
  other arithmetic  5.31 us (9%)
  between operations  1.84 us (3%)
    ppermute x12, starting transfers between devices, passed_along(): return lax.ppermute(block, axis, route)  31.6 us
    ppermute x12, waiting for transfers between devices, passed_along(): return lax.ppermute(block, axis, route)  17.2 us
    unnamed x47, local copies, waits for them, and re-layouts  3.04 us
    unnamed x84, other arithmetic  1.84 us
    reduce_sum x3, other arithmetic, moments(): parts.append(jnp.sum(column[:, None, None, None] * dist, axis=0))  1.36 us
  transfers between devices with their start and end apart: 12, of which 6 were waited for; matrix products, arithmetic and copies ran while one was open for 1% of the time, Pallas kernels for 0%

commit v1 on v0

v1 whole, which is shorter than its diff:
```python
import functools

import jax
import jax.numpy as jnp
import numpy as np
from jax import lax
from jax.experimental import pallas as pl
from jax.experimental.pallas import tpu as pltpu
from jax.sharding import PartitionSpec as P

AXES = ("gx", "gy", "gz")
VEL = [
    (0, 0, 0),
    (1, 0, 0), (-1, 0, 0), (0, 1, 0), (0, -1, 0), (0, 0, 1), (0, 0, -1),
    (1, 1, 0), (-1, -1, 0), (1, -1, 0), (-1, 1, 0),
    (1, 0, 1), (-1, 0, -1), (1, 0, -1), (-1, 0, 1),
    (0, 1, 1), (0, -1, -1), (0, 1, -1), (0, -1, 1),
]
IDX = {v: i for i, v in enumerate(VEL)}
NQ = len(VEL)
OPP = [IDX[tuple(-a for a in v)] for v in VEL]
PAIRS = [(i, OPP[i]) for i in range(1, NQ) if i < OPP[i]]
NA = 5
NV = NQ + NA


def mirror(i, axis):
    v = list(VEL[i])
    v[axis] = -v[axis]
    return IDX[tuple(v)]


UP = [[i for i in range(NQ) if VEL[i][a] == 1] for a in range(3)]
DN = [[mirror(i, a) for i in UP[a]] for a in range(3)]
LV = [[i for i in range(NQ) if VEL[i][a] == 0] for a in range(3)]
AUX = list(range(NQ, NV))


def weight(i):
    return {0: 1.0 / 3.0, 1: 1.0 / 18.0, 2: 1.0 / 36.0}[sum(abs(c) for c in VEL[i])]


def combine(coefs, parts):
    total = None
    for c, p in zip(coefs, parts):
        if c == 0:
            continue
        if total is None:
            total = p if c > 0 else -p
        else:
            total = total + p if c > 0 else total - p
    return total


def raw_moments(f):
    rho = f[0]
    mom = [None, None, None]
    for i, j in PAIRS:
        rho = rho + (f[i] + f[j])
        diff = f[i] - f[j]
        for a in range(3):
            c = VEL[i][a]
            if c:
                if mom[a] is None:
                    mom[a] = diff if c > 0 else -diff
                else:
                    mom[a] = mom[a] + diff if c > 0 else mom[a] - diff
    return rho, mom


class Site:
    def __init__(self, f, aux):
        code, relax, vin = aux[0], aux[1], aux[2:]
        rho, mom = raw_moments(f)
        fluid = code == 2.0
        inlet = code == 3.0
        self.wall = code == 1.0
        self.keep = jnp.where(fluid, 1.0 - relax, 0.0)
        gain = jnp.where(fluid, relax, jnp.where(code > 2.5, 1.0, 0.0))
        r = jnp.where(code == 4.0, 1.0, rho)
        self.u3 = [3.0 * jnp.where(inlet, v, m) for v, m in zip(vin, mom)]
        sq = self.u3[0] * self.u3[0] + self.u3[1] * self.u3[1] + self.u3[2] * self.u3[2]
        self.base = r - sq * (1.0 / 6.0)
        self.gain = {w: gain * w for w in (1.0 / 3.0, 1.0 / 18.0, 1.0 / 36.0)}

    def post(self, vel, wgt, f, f_opp):
        a = combine(vel, self.u3)
        s = self.base if a is None else self.base + (0.5 * a * a + a)
        return jnp.where(self.wall, f_opp, self.keep * f + self.gain[wgt] * s)

    def post_pair(self, vel, wgt, f, f_opp):
        a = combine(vel, self.u3)
        s = self.base + 0.5 * a * a
        g = self.gain[wgt]
        return (
            jnp.where(self.wall, f_opp, self.keep * f + g * (s + a)),
            jnp.where(self.wall, f, self.keep * f_opp + g * (s - a)),
        )

    def post_all(self, f):
        out = [None] * NQ
        out[0] = self.post(VEL[0], weight(0), f[0], f[0])
        for i, j in PAIRS:
            out[i], out[j] = self.post_pair(VEL[i], weight(i), f[i], f[j])
        return out


def odd_mask(axis, shape):
    return jnp.full(shape, lax.rem(lax.axis_index(axis), 2), jnp.int32) == 1


def side_masks(axis, size, shape):
    me = lax.axis_index(axis)
    index = jnp.full(shape, me, jnp.int32)
    return index > 0, index < size - 1


def halves(even, odd, axis, size, shape):
    is_odd = odd_mask(axis, shape)
    low, high = side_masks(axis, size, shape)

    def pick(e, o):
        if o is None:
            return (
                jnp.where(low & is_odd, e, 0.0),
                jnp.where(high & ~is_odd, e, 0.0),
            )
        return (
            jnp.where(low, jnp.where(is_odd, e, o), 0.0),
            jnp.where(high, jnp.where(is_odd, o, e), 0.0),
        )

    return pick


def iota(shape, axis):
    return lax.broadcasted_iota(jnp.int32, shape, axis)


def roll(x, shift, axis):
    shift = shift % x.shape[axis]
    return x if shift == 0 else pltpu.roll(x, shift, axis)


def first_kernel(two, dist, kinds, relax, inflow, post, code, xe, *xo):
    lx, ly, lz = dist.shape[1:]
    for x in range(lx):
        c = kinds[x].astype(jnp.float32) + 1.0
        code[x] = c
        f = [dist[i, x] for i in range(NQ)]
        aux = [c, relax[x]] + [inflow[a, x] for a in range(3)]
        for i, p in enumerate(Site(f, aux).post_all(f)):
            post[i, x] = p

    def value(v, x):
        if v < NQ:
            return post[v, x]
        return [code, relax][v - NQ][x] if v < NQ + 2 else inflow[v - NQ - 2, x]

    is_odd = odd_mask("gx", (ly, lz))
    up = [(i, lx - 2) for i in UP[0]] + [(i, lx - 1) for i in UP[0] + LV[0] + AUX]
    down = [(i, 1) for i in DN[0]] + [(i, 0) for i in DN[0] + LV[0] + AUX]
    for k, (u, d) in enumerate(zip(up, down)):
        to_up, to_down = value(*u), value(*d)
        xe[k] = jnp.where(is_odd, to_down, to_up)
        if two:
            xo[0][k] = jnp.where(is_odd, to_up, to_down)


def plane_value(post, code, relax, inflow, halo):
    lx = post.shape[1]
    n = len(UP[0])

    def value(v, x):
        if v >= NQ:
            if x < 0:
                return halo[0, n + len(UP[0]) + len(LV[0]) + v - NQ]
            if x >= lx:
                return halo[1, n + len(UP[0]) + len(LV[0]) + v - NQ]
            return [code, relax][v - NQ][x] if v < NQ + 2 else inflow[v - NQ - 2, x]
        c = VEL[v][0]
        if c == 0:
            if x < 0:
                return halo[0, 2 * n + LV[0].index(v)]
            if x >= lx:
                return halo[1, 2 * n + LV[0].index(v)]
            return post[v, x]
        if 0 <= x - c < lx:
            return post[v, x - c]
        if c > 0:
            return halo[0, (n if x == 0 else 0) + UP[0].index(v)]
        return halo[1, (n if x == lx - 1 else 0) + DN[0].index(v)]

    return value


Y_UP = [(i, 2) for i in UP[1]] + [(i, 1) for i in UP[1] + LV[1] + AUX]
Y_DN = [(i, 2) for i in DN[1]] + [(i, 1) for i in DN[1] + LV[1] + AUX]


def second_kernel(nx, two_x, two_y, post, code, relax, inflow, *refs):
    refs = list(refs)
    re = refs.pop(0)
    ro = refs.pop(0) if two_x else None
    halo, ye = refs.pop(0), refs.pop(0)
    yo = refs.pop(0) if two_y else None
    lx, ly, lz = post.shape[1:]
    shape = (ly, lz)
    pick = halves(re, ro, "gx", nx, shape)
    for k in range(re.shape[0]):
        low, high = pick(re[k], None if ro is None else ro[k])
        halo[0, k] = low
        halo[1, k] = high
    value = plane_value(post, code, relax, inflow, halo)
    row = iota(shape, 0)
    is_odd = odd_mask("gy", shape)
    planes = lx + 2
    per = ly // planes
    for t in range(NV // per):
        up = down = None
        for h in range(per):
            (u, du), (d, dd) = Y_UP[per * t + h], Y_DN[per * t + h]
            for x in range(planes):
                j = h * planes + x
                a = roll(value(u, x - 1), j - (ly - du), 0)
                b = roll(value(d, x - 1), j - (dd - 1), 0)
                up = a if up is None else jnp.where(row == j, a, up)
                down = b if down is None else jnp.where(row == j, b, down)
        ye[t] = jnp.where(is_odd, down, up)
        if two_y:
            yo[t] = jnp.where(is_odd, up, down)


def third_kernel(ny, two_y, two_z, post, code, relax, inflow, halo, *refs):
    refs = list(refs)
    ye = refs.pop(0)
    yo = refs.pop(0) if two_y else None
    re = refs.pop(0)
    ro = refs.pop(0) if two_y else None
    moved, ze = refs.pop(0), refs.pop(0)
    zo = refs.pop(0) if two_z else None
    lx, ly, lz = post.shape[1:]
    shape = (ly, lz)
    value = plane_value(post, code, relax, inflow, halo)
    row = iota(shape, 0)
    planes = lx + 2
    per = ly // planes
    is_odd = odd_mask("gy", shape)
    pick = halves(re, ro, "gy", ny, shape)
    tiles = NV // per
    got_low, got_high, own_up, own_down = [], [], [], []
    for t in range(tiles):
        low, high = pick(re[t], None if ro is None else ro[t])
        got_low.append(low)
        got_high.append(high)
        e = ye[t]
        o = e if yo is None else yo[t]
        own_up.append(jnp.where(is_odd, o, e))
        own_down.append(jnp.where(is_odd, e, o))
    if yo is None:
        for t in range(tiles):
            up = down = None
            for h in range(per):
                (u, du), (d, dd) = Y_UP[per * t + h], Y_DN[per * t + h]
                for x in range(planes):
                    j = h * planes + x
                    a = roll(value(u, x - 1), j - (ly - du), 0)
                    b = roll(value(d, x - 1), j - (dd - 1), 0)
                    up = a if up is None else jnp.where(row == j, a, up)
                    down = b if down is None else jnp.where(row == j, b, down)
            own_up[t], own_down[t] = up, down

    def group(tiles_of, slot, dst):
        return roll(tiles_of[slot // per], (dst - slot % per) * planes, 0)

    first = row < planes
    n = len(UP[1])
    for v in range(NV):
        c = VEL[v][1] if v < NQ else 0
        if c > 0:
            p = UP[1].index(v)
            edge = jnp.where(first, group(got_low, p, 0), group(own_up, n + p, 1))
        elif c < 0:
            p = DN[1].index(v)
            edge = jnp.where(first, group(own_down, n + p, 0), group(got_high, p, 1))
        else:
            p = 2 * n + (LV[1].index(v) if v < NQ else len(LV[1]) + v - NQ)
            edge = jnp.where(first, group(got_low, p, 0), group(got_high, p, 1))
        moved[v, planes] = edge
        for x in range(planes):
            q = value(v, x - 1)
            if c > 0:
                s = n + UP[1].index(v)
                line = roll(got_low[s // per], -((s % per) * planes + x), 0)
                q = jnp.where(row == 0, line, roll(q, 1, 0))
            elif c < 0:
                s = n + DN[1].index(v)
                line = roll(got_high[s // per], ly - 1 - ((s % per) * planes + x), 0)
                q = jnp.where(row == ly - 1, line, roll(q, -1, 0))
            moved[v, x] = q

    lanes = 128
    small = (ly, lanes)
    lane = iota(small, 1)
    up = jnp.zeros(small, jnp.float32)
    down = jnp.zeros(small, jnp.float32)
    n = len(UP[2])
    for t in range(planes + 1):
        for p, (u, d) in enumerate(zip(UP[2], DN[2])):
            at = NV * t + 2 * p
            here = (lane == at) | (lane == at + 1)
            up = jnp.where(here, roll(moved[u, t, :, lz - lanes :], at - (lanes - 2), 1), up)
            down = jnp.where(here, roll(moved[d, t, :, :lanes], at, 1), down)
        for q, v in enumerate(LV[2] + AUX):
            at = NV * t + 2 * n + q
            here = lane == at
            up = jnp.where(here, roll(moved[v, t, :, lz - lanes :], at - (lanes - 1), 1), up)
            down = jnp.where(here, roll(moved[v, t, :, :lanes], at, 1), down)
    is_odd = odd_mask("gz", small)
    ze[...] = jnp.where(is_odd, down, up)
    if two_z:
        zo[...] = jnp.where(is_odd, up, down)


def final_moments(moved, lx):
    planes = lx + 2
    post = {}
    for t in range(planes):
        f = [roll(moved(i, t), VEL[i][2], 1) for i in range(NQ)]
        site = Site(f, [moved(v, t) for v in AUX])
        if t == 0 or t == planes - 1:
            for i in UP[0] if t == 0 else DN[0]:
                post[i, t] = site.post(VEL[i], weight(i), f[i], f[OPP[i]])
        else:
            for i, p in enumerate(site.post_all(f)):
                post[i, t] = p
    t = planes
    f = [roll(moved(i, t), VEL[i][2], 1) for i in range(NQ)]
    site = Site(f, [moved(v, t) for v in AUX])
    shape = f[0].shape
    ly = shape[0]
    row = iota(shape, 0)
    first = row < planes
    site.u3[1] = jnp.where(first, site.u3[1], -site.u3[1])
    edge = {}
    for u, d in zip(UP[1], DN[1]):
        edge[VEL[u][0], VEL[u][2]] = site.post(
            VEL[u],
            weight(u),
            jnp.where(first, f[u], f[d]),
            jnp.where(first, f[OPP[u]], f[OPP[d]]),
        )

    def shifted(main, cy, lines):
        at, base = (0, 0) if cy > 0 else (ly - 1, planes)
        line = combine([s for s, _, _ in lines], [roll(e, at - (base + p), 0) for _, e, p in lines])
        return jnp.where(row == at, line, roll(main, cy, 0))

    result = []
    for t in range(1, lx + 1):

        def get(cx, cy, cz):
            return post[IDX[cx, cy, cz], t - cx]

        density = get(0, 0, 0) + get(1, 0, 0) + get(-1, 0, 0)
        mx = get(1, 0, 0) - get(-1, 0, 0)
        my = None
        for cy in (1, -1):
            centre, plus, minus = get(0, cy, 0), get(1, cy, 0), get(-1, cy, 0)
            ec, ep, em = edge[0, 0], edge[1, 0], edge[-1, 0]
            total = shifted(centre + (plus + minus), cy, [(1, ec, t), (1, ep, t - 1), (1, em, t + 1)])
            mx = mx + shifted(plus - minus, cy, [(1, ep, t - 1), (-1, em, t + 1)])
            density = density + total
            my = total if my is None else my - total
        mz = None
        for cz in (1, -1):
            plus, minus = get(1, 0, cz), get(-1, 0, cz)
            a = shifted(get(0, 1, cz), 1, [(1, edge[0, cz], t)])
            b = shifted(get(0, -1, cz), -1, [(1, edge[0, cz], t)])
            total = roll(get(0, 0, cz) + (plus + minus) + (a + b), cz, 1)
            mx = mx + roll(plus - minus, cz, 1)
            my = my + roll(a - b, cz, 1)
            density = density + total
            mz = total if mz is None else mz - total
        result.append([density, mx, my, mz])
    return result


def last_kernel(nz, two_z, moved, *refs):
    refs = list(refs)
    re = refs.pop(0)
    ro = refs.pop(0) if two_z else None
    density, momentum = refs
    planes = moved.shape[1] - 1
    lx = planes - 2
    ly, lz = moved.shape[2:]
    lanes = 128
    small = (ly, lanes)
    lane = iota(small, 1)
    low, high = halves(re, ro, "gz", nz, small)(re[...], None if ro is None else ro[...])
    n = len(UP[2])
    half, most = lanes // 2, lanes - lanes // 4

    def seam(v, t):
        x = jnp.where(lane < most, roll(moved[v, t, :, :lanes], half, 1), moved[v, t, :, lz - lanes :])
        c = VEL[v][2] if v < NQ else 0
        if c > 0:
            at = NV * t + 2 * UP[2].index(v)
            return jnp.where((lane == half - 1) | (lane == half - 2), roll(low, half - 2 - at, 1), x)
        if c < 0:
            at = NV * t + 2 * DN[2].index(v)
            return jnp.where(lane < 2, roll(high, -at, 1), x)
        at = NV * t + 2 * n + (LV[2].index(v) if v < NQ else len(LV[2]) + v - NQ)
        x = jnp.where(lane == half - 1, roll(low, half - 1 - at, 1), x)
        return jnp.where(lane == 0, roll(high, -at, 1), x)

    inner = final_moments(lambda v, t: moved[v, t], lx)
    rim = final_moments(seam, lx)
    for x in range(lx):
        for a in range(4):
            main, edge = inner[x][a], rim[x][a]
            parts = [main[:, k * lanes : (k + 1) * lanes] for k in range(lz // lanes)]
            parts[0] = jnp.where(lane < 2, roll(edge, -half, 1), parts[0])
            parts[-1] = jnp.where(lane >= lanes - 2, edge, parts[-1])
            for k, p in enumerate(parts):
                if a == 0:
                    density[x, :, k * lanes : (k + 1) * lanes] = p
                else:
                    momentum[a - 1, x, :, k * lanes : (k + 1) * lanes] = p


def pair_routes(sizes):
    def linear(c):
        return (c[0] * sizes[1] + c[1]) * sizes[2] + c[2]

    routes = []
    for axis in range(3):
        own = []
        for odd in range(2 if sizes[axis] > 2 else 1):
            spare = [a for a in (1, 2, 0) if a != axis and sizes[a] % 2 == 0]
            route = []
            for c in np.ndindex(*sizes):
                other = list(c)
                k = ((c[axis] - odd) ^ 1) + odd
                if 0 <= k < sizes[axis]:
                    other[axis] = k
                elif spare:
                    other[spare[0]] ^= 1
                else:
                    continue
                route.append((linear(c), linear(other)))
            own.append(route)
        routes.append(own)
    return routes


def swap(messages, routes):
    return [lax.ppermute(m, AXES, r) for m, r in zip(messages, routes)]


def call(body, outs, flops, *args):
    size = sum(int(np.prod(a.shape)) * 4 for a in args) + sum(int(np.prod(s)) * 4 for s in outs)
    return pl.pallas_call(
        body,
        out_shape=[jax.ShapeDtypeStruct(s, jnp.float32) for s in outs],
        in_specs=[pl.BlockSpec(memory_space=pltpu.VMEM)] * len(args),
        out_specs=[pl.BlockSpec(memory_space=pltpu.VMEM)] * len(outs),
        cost_estimate=pl.CostEstimate(flops=flops, bytes_accessed=size, transcendentals=0),
    )(*args)


def shards(sizes, dist, site_kinds, relax, inflow):
    lx, ly, lz = dist.shape[1:]
    routes = pair_routes(sizes)
    two = [len(r) == 2 for r in routes]
    planes = lx + 2
    block = lx * ly * lz
    xs, ys = (NV, ly, lz), (NV * planes // ly, ly, lz)
    post, code, *xm = call(
        functools.partial(first_kernel, two[0]),
        [dist.shape, site_kinds.shape] + [xs] * len(routes[0]),
        250 * block,
        dist, site_kinds, relax, inflow,
    )
    xr = swap(xm, routes[0])
    halo, *ym = call(
        functools.partial(second_kernel, sizes[0], two[0], two[1]),
        [(2,) + xs] + [ys] * len(routes[1]),
        100 * block,
        post, code, relax, inflow, *xr,
    )
    yr = swap(ym, routes[1])
    moved, *zm = call(
        functools.partial(third_kernel, sizes[1], two[1], two[2]),
        [(NV, planes + 1, ly, lz)] + [(ly, 128)] * len(routes[2]),
        100 * block,
        post, code, relax, inflow, halo, *ym, *yr,
    )
    zr = swap(zm, routes[2])
    density, momentum = call(
        functools.partial(last_kernel, sizes[2], two[2]),
        [(lx, ly, lz), (3, lx, ly, lz)],
        400 * block,
        moved, *zr,
    )
    return density, momentum


def solution(mesh):
    sizes = tuple(mesh.shape[a] for a in AXES)
    return jax.shard_map(
        functools.partial(shards, sizes),
        mesh=mesh,
        in_specs=(
            P(None, "gx", "gy", "gz"),
            P("gx", "gy", "gz"),
            P("gx", "gy", "gz"),
            P(None, "gx", "gy", "gz"),
        ),
        out_specs=(P("gx", "gy", "gz"), P(None, "gx", "gy", "gz")),
        check_vma=False,
    )
```

time: 62 us -> 30.8 us (0.50)
  the two profiles are of different devices: /device:TPU:10 before, /device:TPU:0 now
where the time goes in v1:
time: 30.8 us; the launch traced here: 30.6 us
  Pallas kernels  11.1 us (36%)
  waiting for transfers between devices  10.4 us (34%)
  starting transfers between devices  6.43 us (21%)
  local copies, waits for them, and re-layouts  1.96 us (6%)
  between operations  0.64 us (2%)
    pallas_call x4, Pallas kernels, call(): pl.pallas_call(body, out_shape=[jax.ShapeDtypeStruct(s, jnp.float32) for...  11.1 us
    ppermute x5, waiting for transfers between devices, swap(): return [lax.ppermute(m, AXES, r) for m, r in zip(messages, routes)]  10.4 us
    ppermute x5, starting transfers between devices, swap(): return [lax.ppermute(m, AXES, r) for m, r in zip(messages, routes)]  6.43 us
    unnamed x10, local copies, waits for them, and re-layouts  1.96 us
  transfers between devices with their start and end apart: 5, of which 3 were waited for; matrix products, arithmetic and copies ran while one was open for 0% of the time, Pallas kernels for 0%

profile of v1, /device:TPU:0, one launch (start us, length us, event | category | flops | bytes accessed | tf_op | source)
XLA Modules:
  0.0 30.6 jit_solution(16973517379765230633)
XLA Ops:
  0.6 2.0 %shard_map.59 = (f32[19,2,8,256]{3,2,1,0:T(8,128)}, f32[2,8,256]{2,1,0:T(8,128)}, f32[24,8,256]{2,1,0:T(8,128)}, f32[24,8,256]{2,1,0:T(8,128)}) custom-call(f32[19,2,8,256]{3,2,1,0:T(8,128)} %dist.1, s32[2,8,256]{2,1,0:T(8,128)} %kinds.1, f32[2,8,256]{2,1,0:T(8,128)} %relax.5, f32[3,2,8,256]{3,2,1,0:T(8,128)} %inflow.5), custom_call_target="tpu_custom_call" | custom-call | flops 1024000 | bytes 1114112 | tf_op jit(solution)/shard_map/pallas_call | solution.py:463
  2.6 3.1 %collective-permute-start = (f32[24,8,256]{2,1,0:T(8,128)}, f32[24,8,256]{2,1,0:T(8,128)S(1)}, u32[]{:S(2)}, u32[]{:S(2)}) collective-permute-start(f32[24,8,256]{2,1,0:T(8,128)} %get-tuple-element.13), channel_id=1, source_target_pairs={{0,8},{1,9},{2,10},{3,11},{4,12},{5,13},{6,14},{7,15},{8,0},{9,1},... | collective-permute-start | bytes 589832 | tf_op jit(solution)/shard_map/ppermute | solution.py:458
  5.7 0.0 collective-permute-start.1
  5.7 5.1 %collective-permute-done.refs_0_ = f32[24,8,256]{2,1,0:T(8,128)S(1)} collective-permute-done((f32[24,8,256]{2,1,0:T(8,128)}, f32[24,8,256]{2,1,0:T(8,128)S(1)}, u32[]{:S(2)}, u32[]{:S(2)}) %collective-permute-start) | collective-permute-done | bytes 196640 | tf_op jit(solution)/shard_map/ppermute | solution.py:458
  10.8 0.0 copy-start
  10.8 0.0 collective-permute-done.1.refs_1_
  10.8 0.0 copy-start.1
  10.8 0.7 %copy-done = f32[24,8,256]{2,1,0:T(8,128)} copy-done((f32[24,8,256]{2,1,0:T(8,128)}, f32[24,8,256]{2,1,0:T(8,128)S(1)}, u32[]{:S(2)}) %copy-start) | copy-done | bytes 196632
  11.4 0.1 copy-done.1
  11.5 2.1 %shard_map.60 = (f32[2,24,8,256]{3,2,1,0:T(8,128)}, f32[12,8,256]{2,1,0:T(8,128)}, f32[12,8,256]{2,1,0:T(8,128)}) custom-call(f32[19,2,8,256]{3,2,1,0:T(8,128)} %get-tuple-element.11.post, f32[2,8,256]{2,1,0:T(8,128)} %get-tuple-element.12.code, f32[2,8,256]{2,1,0:T(8,128)} %relax.5, f32[3,2,8,256]{3,2,1,0:T(8,128)} %inflow.5, f32[24,8,256]{2,1,0:T(8,128)} %copy-done, ...), custom_call_target="tpu_custom_call" | custom-call | flops 409600 | bytes 1376256 | tf_op jit(solution)/shard_map/pallas_call | solution.py:463
  13.6 0.0 collective-permute-start.2
  13.6 1.7 %collective-permute-start.3 = (f32[12,8,256]{2,1,0:T(8,128)}, f32[12,8,256]{2,1,0:T(8,128)S(1)}, u32[]{:S(2)}, u32[]{:S(2)}) collective-permute-start(f32[12,8,256]{2,1,0:T(8,128)} %get-tuple-element.17.refs_1_), channel_id=1, source_target_pairs={{0,1},{1,0},{2,4},{3,5},{4,2},{5,3},{6,7},{7,6},{8,9},{9,8},{10,12... | collective-permute-start | bytes 294920 | tf_op jit(solution)/shard_map/ppermute | solution.py:458
  15.3 0.0 collective-permute-done.2.refs_2_
  15.3 0.0 copy-start.2
  15.3 3.1 %collective-permute-done.3.refs_3_ = f32[12,8,256]{2,1,0:T(8,128)S(1)} collective-permute-done((f32[12,8,256]{2,1,0:T(8,128)}, f32[12,8,256]{2,1,0:T(8,128)S(1)}, u32[]{:S(2)}, u32[]{:S(2)}) %collective-permute-start.3) | collective-permute-done | bytes 98336 | tf_op jit(solution)/shard_map/ppermute | solution.py:458
  18.4 0.0 copy-start.3
  18.4 0.0 copy-done.2
  18.4 0.6 %copy-done.3 = f32[12,8,256]{2,1,0:T(8,128)} copy-done((f32[12,8,256]{2,1,0:T(8,128)}, f32[12,8,256]{2,1,0:T(8,128)S(1)}, u32[]{:S(2)}) %copy-start.3) | copy-done | bytes 98328
  19.1 2.5 %shard_map.61 = (f32[24,5,8,256]{3,2,1,0:T(8,128)}, f32[8,128]{1,0:T(8,128)}) custom-call(f32[19,2,8,256]{3,2,1,0:T(8,128)} %get-tuple-element.11.post, f32[2,8,256]{2,1,0:T(8,128)} %get-tuple-element.12.code, f32[2,8,256]{2,1,0:T(8,128)} %relax.5, f32[3,2,8,256]{3,2,1,0:T(8,128)} %inflow.5, f32[2,24,8,256]{3,2,1,0:T(8,128)} %get-tuple-element.15.halo, ...), custom_call_target="tpu_custom_call" | custom-call | flops 409600 | bytes 2166784 | tf_op jit(solution)/shard_map/pallas_call | solution.py:463
  21.5 1.7 %collective-permute-start.4 = (f32[8,128]{1,0:T(8,128)}, f32[8,128]{1,0:T(8,128)S(1)}, u32[]{:S(2)}, u32[]{:S(2)}) collective-permute-start(f32[8,128]{1,0:T(8,128)} %get-tuple-element.19), channel_id=1, source_target_pairs={{0,1},{1,0},{2,3},{3,2},{4,5},{5,4},{6,7},{7,6},{8,9},{9,8},{10,11... | collective-permute-start | bytes 12296 | tf_op jit(solution)/shard_map/ppermute | solution.py:458
  23.2 2.1 %collective-permute-done.4.refs_0_ = f32[8,128]{1,0:T(8,128)S(1)} collective-permute-done((f32[8,128]{1,0:T(8,128)}, f32[8,128]{1,0:T(8,128)S(1)}, u32[]{:S(2)}, u32[]{:S(2)}) %collective-permute-start.4) | collective-permute-done | bytes 4128 | tf_op jit(solution)/shard_map/ppermute | solution.py:458
  25.3 0.0 copy-start.4
  25.3 0.6 %copy-done.4 = f32[8,128]{1,0:T(8,128)} copy-done((f32[8,128]{1,0:T(8,128)}, f32[8,128]{1,0:T(8,128)S(1)}, u32[]{:S(2)}) %copy-start.4) | copy-done | bytes 4120
  25.9 4.6 %shard_map.62 = (f32[2,8,256]{2,1,0:T(8,128)}, f32[3,2,8,256]{3,2,1,0:T(8,128)}) custom-call(f32[24,5,8,256]{3,2,1,0:T(8,128)} %get-tuple-element.18.moved, f32[8,128]{1,0:T(8,128)} %copy-done.4), custom_call_target="tpu_custom_call" | custom-call | flops 1638400 | bytes 1052672 | tf_op jit(solution)/shard_map/pallas_call | solution.py:463
Async XLA Ops:
  2.6 8.2 %collective-permute-start = (f32[24,8,256]{2,1,0:T(8,128)}, f32[24,8,256]{2,1,0:T(8,128)S(1)}, u32[]{:S(2)}, u32[]{:S(2)}) collective-permute-start(f32[24,8,256]{2,1,0:T(8,128)} %get-tuple-element.13), channel_id=1, source_target_pairs={{0,8},{1,9},{2,10},{3,11},{4,12},{5,13},{6,14},{7,15},{8,0},{9,1},... | collective-permute-start | bytes 589832 | tf_op jit(solution)/shard_map/ppermute | solution.py:458
  5.7 5.1 %collective-permute-start.1 = (f32[24,8,256]{2,1,0:T(8,128)}, f32[24,8,256]{2,1,0:T(8,128)S(1)}, u32[]{:S(2)}, u32[]{:S(2)}) collective-permute-start(f32[24,8,256]{2,1,0:T(8,128)} %get-tuple-element.14), channel_id=1, source_target_pairs={{0,2},{1,3},{2,0},{3,1},{4,6},{5,7},{6,4},{7,5},{8,16},{9,17},{10,... | collective-permute-start | bytes 589832 | tf_op jit(solution)/shard_map/ppermute | solution.py:458
  10.8 0.7 %copy-start = (f32[24,8,256]{2,1,0:T(8,128)}, f32[24,8,256]{2,1,0:T(8,128)S(1)}, u32[]{:S(2)}) copy-start(f32[24,8,256]{2,1,0:T(8,128)S(1)} %collective-permute-done.refs_0_) | copy-start | bytes 589828
  10.8 0.7 %copy-start.1 = (f32[24,8,256]{2,1,0:T(8,128)}, f32[24,8,256]{2,1,0:T(8,128)S(1)}, u32[]{:S(2)}) copy-start(f32[24,8,256]{2,1,0:T(8,128)S(1)} %collective-permute-done.1.refs_1_) | copy-start | bytes 589828
  13.6 1.7 %collective-permute-start.2 = (f32[12,8,256]{2,1,0:T(8,128)}, f32[12,8,256]{2,1,0:T(8,128)S(1)}, u32[]{:S(2)}, u32[]{:S(2)}) collective-permute-start(f32[12,8,256]{2,1,0:T(8,128)} %get-tuple-element.16.refs_0_), channel_id=1, source_target_pairs={{0,2},{1,3},{2,0},{3,1},{4,6},{5,7},{6,4},{7,5},{8,10},{9,11},{10,... | collective-permute-start | bytes 294920 | tf_op jit(solution)/shard_map/ppermute | solution.py:458
  13.6 4.8 %collective-permute-start.3 = (f32[12,8,256]{2,1,0:T(8,128)}, f32[12,8,256]{2,1,0:T(8,128)S(1)}, u32[]{:S(2)}, u32[]{:S(2)}) collective-permute-start(f32[12,8,256]{2,1,0:T(8,128)} %get-tuple-element.17.refs_1_), channel_id=1, source_target_pairs={{0,1},{1,0},{2,4},{3,5},{4,2},{5,3},{6,7},{7,6},{8,9},{9,8},{10,12... | collective-permute-start | bytes 294920 | tf_op jit(solution)/shard_map/ppermute | solution.py:458
  15.3 3.1 %copy-start.2 = (f32[12,8,256]{2,1,0:T(8,128)}, f32[12,8,256]{2,1,0:T(8,128)S(1)}, u32[]{:S(2)}) copy-start(f32[12,8,256]{2,1,0:T(8,128)S(1)} %collective-permute-done.2.refs_2_) | copy-start | bytes 294916
  18.4 0.6 %copy-start.3 = (f32[12,8,256]{2,1,0:T(8,128)}, f32[12,8,256]{2,1,0:T(8,128)S(1)}, u32[]{:S(2)}) copy-start(f32[12,8,256]{2,1,0:T(8,128)S(1)} %collective-permute-done.3.refs_3_) | copy-start | bytes 294916
  21.5 3.8 %collective-permute-start.4 = (f32[8,128]{1,0:T(8,128)}, f32[8,128]{1,0:T(8,128)S(1)}, u32[]{:S(2)}, u32[]{:S(2)}) collective-permute-start(f32[8,128]{1,0:T(8,128)} %get-tuple-element.19), channel_id=1, source_target_pairs={{0,1},{1,0},{2,3},{3,2},{4,5},{5,4},{6,7},{7,6},{8,9},{9,8},{10,11... | collective-permute-start | bytes 12296 | tf_op jit(solution)/shard_map/ppermute | solution.py:458
  25.3 0.6 %copy-start.4 = (f32[8,128]{1,0:T(8,128)}, f32[8,128]{1,0:T(8,128)S(1)}, u32[]{:S(2)}) copy-start(f32[8,128]{1,0:T(8,128)S(1)} %collective-permute-done.4.refs_0_) | copy-start | bytes 12292

commit v2 on v1

v2 whole, which is shorter than its diff:
```python
import functools

import jax
import jax.numpy as jnp
import numpy as np
from jax import lax
from jax.experimental import pallas as pl
from jax.experimental.pallas import tpu as pltpu
from jax.sharding import PartitionSpec as P


AXES = ("gx", "gy", "gz")
VEL = [
    (0, 0, 0),
    (1, 0, 0), (-1, 0, 0), (0, 1, 0), (0, -1, 0), (0, 0, 1), (0, 0, -1),
    (1, 1, 0), (-1, -1, 0), (1, -1, 0), (-1, 1, 0),
    (1, 0, 1), (-1, 0, -1), (1, 0, -1), (-1, 0, 1),
    (0, 1, 1), (0, -1, -1), (0, 1, -1), (0, -1, 1),
]
IDX = {v: i for i, v in enumerate(VEL)}
NQ = len(VEL)
OPP = [IDX[tuple(-a for a in v)] for v in VEL]
PAIRS = [(i, OPP[i]) for i in range(1, NQ) if i < OPP[i]]
NA = 5
NV = NQ + NA
LANES = 128


def mirror(i, axis):
    v = list(VEL[i])
    v[axis] = -v[axis]
    return IDX[tuple(v)]


UP = [[i for i in range(NQ) if VEL[i][a] == 1] for a in range(3)]
DN = [[mirror(i, a) for i in UP[a]] for a in range(3)]
LV = [[i for i in range(NQ) if VEL[i][a] == 0] for a in range(3)]
AUX = list(range(NQ, NV))


def weight(i):
    return {0: 1.0 / 3.0, 1: 1.0 / 18.0, 2: 1.0 / 36.0}[sum(abs(c) for c in VEL[i])]


def combine(coefs, parts):
    total = None
    for c, p in zip(coefs, parts):
        if c == 0:
            continue
        if total is None:
            total = p if c > 0 else -p
        else:
            total = total + p if c > 0 else total - p
    return total


def raw_moments(f):
    rho = f[0]
    mom = [None, None, None]
    for i, j in PAIRS:
        rho = rho + (f[i] + f[j])
        diff = f[i] - f[j]
        for a in range(3):
            c = VEL[i][a]
            if c:
                if mom[a] is None:
                    mom[a] = diff if c > 0 else -diff
                else:
                    mom[a] = mom[a] + diff if c > 0 else mom[a] - diff
    return rho, mom


class Site:
    def __init__(self, f, aux):
        code, relax, vin = aux[0], aux[1], aux[2:]
        rho, mom = raw_moments(f)
        fluid = code == 2.0
        inlet = code == 3.0
        self.wall = code == 1.0
        self.keep = jnp.where(fluid, 1.0 - relax, 0.0)
        gain = jnp.where(fluid, relax, jnp.where(code > 2.5, 1.0, 0.0))
        r = jnp.where(code == 4.0, 1.0, rho)
        self.u3 = [3.0 * jnp.where(inlet, v, m) for v, m in zip(vin, mom)]
        sq = self.u3[0] * self.u3[0] + self.u3[1] * self.u3[1] + self.u3[2] * self.u3[2]
        self.base = r - sq * (1.0 / 6.0)
        self.gain = {w: gain * w for w in (1.0 / 3.0, 1.0 / 18.0, 1.0 / 36.0)}

    def post(self, vel, wgt, f, f_opp):
        a = combine(vel, self.u3)
        s = self.base if a is None else self.base + (0.5 * a * a + a)
        return jnp.where(self.wall, f_opp, self.keep * f + self.gain[wgt] * s)

    def post_pair(self, vel, wgt, f, f_opp):
        a = combine(vel, self.u3)
        s = self.base + 0.5 * a * a
        g = self.gain[wgt]
        return (
            jnp.where(self.wall, f_opp, self.keep * f + g * (s + a)),
            jnp.where(self.wall, f, self.keep * f_opp + g * (s - a)),
        )

    def post_all(self, f):
        out = [None] * NQ
        out[0] = self.post(VEL[0], weight(0), f[0], f[0])
        for i, j in PAIRS:
            out[i], out[j] = self.post_pair(VEL[i], weight(i), f[i], f[j])
        return out


    def edge_rows(self, f, first):
        self.u3[1] = jnp.where(first, self.u3[1], -self.u3[1])
        edge = {}
        for u, d in zip(UP[1], DN[1]):
            edge[VEL[u][0], VEL[u][2]] = self.post(
                VEL[u],
                weight(u),
                jnp.where(first, f[u], f[d]),
                jnp.where(first, f[OPP[u]], f[OPP[d]]),
            )
        return edge


def odd_mask(axis, shape):
    return jnp.full(shape, lax.rem(lax.axis_index(axis), 2), jnp.int32) == 1


def side_masks(axis, size, shape):
    me = lax.axis_index(axis)
    index = jnp.full(shape, me, jnp.int32)
    return index > 0, index < size - 1


def halves(axis, size, shape):
    is_odd = odd_mask(axis, shape)
    low, high = side_masks(axis, size, shape)

    def pick(e, o):
        if o is None:
            return (
                jnp.where(low & is_odd, e, 0.0),
                jnp.where(high & ~is_odd, e, 0.0),
            )
        return (
            jnp.where(low, jnp.where(is_odd, e, o), 0.0),
            jnp.where(high, jnp.where(is_odd, o, e), 0.0),
        )

    return pick


def iota(shape, axis):
    return lax.broadcasted_iota(jnp.int32, shape, axis)


def roll(x, shift, axis):
    shift = shift % x.shape[axis]
    return x if shift == 0 else pltpu.roll(x, shift, axis)


Y_UP = [(i, 2) for i in UP[1]] + [(i, 1) for i in UP[1] + LV[1] + AUX]
Y_DN = [(i, 2) for i in DN[1]] + [(i, 1) for i in DN[1] + LV[1] + AUX]


def source(v, x, lx):
    c = VEL[v][0] if v < NQ else 0
    x -= c
    if x < 0:
        return 0, x + lx
    if x >= lx:
        return 1, x - lx
    return None, x


def edge_rows(side, lx):
    return [
        (way, k, x)
        for way, slots in enumerate((Y_UP, Y_DN))
        for k, (v, _) in enumerate(slots)
        for x in range(-1, lx + 1)
        if source(v, x, lx)[0] == side
    ]


def row_of(way, k, ly):
    return ly - Y_UP[k][1] if way == 0 else Y_DN[k][1] - 1


def pop_of(way, k):
    return (Y_UP, Y_DN)[way][k][0]


def bulk_planes(side, lx):
    near, far = (-1, 0) if side == 0 else (lx, lx - 1)
    away = (UP, DN)[side][0]
    return [(i, near) for i in away] + [(i, far) for i in away] + [(i, near) for i in LV[0] + AUX]


def gather_rows(rows, ly):
    tiles = []
    for base in range(0, len(rows), ly):
        total = None
        for j, (tile, r) in enumerate(rows[base : base + ly]):
            part = roll(tile, j - r, 0)
            total = part if total is None else jnp.where(iota(part.shape, 0) == j, part, total)
        tiles.append(total)
    return tiles


def first_kernel(two, dist, kinds, relax, inflow, post, aux, *refs):
    refs = list(refs)
    edge = [refs.pop(0) for _ in range(1 + two)]
    bulk = [refs.pop(0) for _ in range(1 + two)]
    dist_v, kinds_v, sems = refs
    copies = [
        pltpu.make_async_copy(kinds, kinds_v, sems.at[0]),
        pltpu.make_async_copy(relax, aux.at[1], sems.at[1]),
        pltpu.make_async_copy(inflow, aux.at[pl.ds(2, 3)], sems.at[2]),
        pltpu.make_async_copy(dist, dist_v, sems.at[3]),
    ]
    for c in copies:
        c.start()
    for c in copies:
        c.wait()
    lx, ly, lz = dist.shape[1:]
    for x in range(lx):
        aux[0, x] = kinds_v[x].astype(jnp.float32) + 1.0
        f = [dist_v[i, x] for i in range(NQ)]
        for i, p in enumerate(Site(f, [aux[a, x] for a in range(NA)]).post_all(f)):
            post[i, x] = p

    def sent(v, x):
        plane = source(v, x, lx)[1]
        return post[v, plane] if v < NQ else aux[v - NQ, plane]

    is_odd = odd_mask("gx", (ly, lz))

    def put(refs, k, to_up, to_down):
        refs[0][k] = jnp.where(is_odd, to_down, to_up)
        if two:
            refs[1][k] = jnp.where(is_odd, to_up, to_down)

    sides = [
        gather_rows([(sent(pop_of(w, k), x), row_of(w, k, ly)) for w, k, x in edge_rows(s, lx)], ly)
        for s in (0, 1)
    ]
    for k, (u, d) in enumerate(zip(*sides)):
        put(edge, k, u, d)
    for k, (u, d) in enumerate(zip(bulk_planes(0, lx), bulk_planes(1, lx))):
        put(bulk, k, sent(*u), sent(*d))


def second_kernel(nx, two_x, post, aux, *refs):
    refs = list(refs)
    re = refs.pop(0)
    ro = refs.pop(0) if two_x else None
    ys = refs
    lx, ly, lz = post.shape[1:]
    pick = halves("gx", nx, (ly, lz))
    got = [pick(re[k], None if ro is None else ro[k]) for k in range(re.shape[0])]
    where = {}
    for side in (0, 1):
        for n, item in enumerate(edge_rows(side, lx)):
            where[item] = (got[n // ly][side], n % ly)
    tiles = []
    for way in (0, 1):
        rows = []
        for k in range(NV):
            v = pop_of(way, k)
            for x in range(-1, lx + 1):
                side, plane = source(v, x, lx)
                if side is not None:
                    rows.append(where[way, k, x])
                else:
                    rows.append((post[v, plane] if v < NQ else aux[v - NQ, plane], row_of(way, k, ly)))
        tiles.append(gather_rows(rows, ly))
    is_odd = odd_mask("gy", (ly, lz))
    for t, (up, down) in enumerate(zip(*tiles)):
        ys[0][t] = jnp.where(is_odd, down, up)
        ys[1][t] = jnp.where(is_odd, up, down)


def third_kernel(nx, ny, two_x, two_y, two_z, post, aux, *refs):
    refs = list(refs)
    xe = refs.pop(0)
    xo = refs.pop(0) if two_x else None
    ys = [refs.pop(0), refs.pop(0)]
    re = refs.pop(0)
    ro = refs.pop(0) if two_y else None
    moved, ze = refs.pop(0), refs.pop(0)
    zo = refs.pop(0) if two_z else None
    lx, ly, lz = post.shape[1:]
    shape = (ly, lz)
    row = iota(shape, 0)
    planes = lx + 2
    per = ly // planes
    pick = halves("gx", nx, shape)
    halo = {}
    for k, (u, d) in enumerate(zip(bulk_planes(0, lx), bulk_planes(1, lx))):
        halo[u], halo[d] = pick(xe[k], None if xo is None else xo[k])

    def value(v, x):
        side, plane = source(v, x, lx)
        if side is not None:
            return halo[v, x]
        return post[v, plane] if v < NQ else aux[v - NQ, plane]

    is_odd = odd_mask("gy", shape)
    pick = halves("gy", ny, shape)
    got_low, got_high, own_up, own_down = [], [], [], []
    for t in range(NV // per):
        low, high = pick(re[t], None if ro is None else ro[t])
        got_low.append(low)
        got_high.append(high)
        e, o = ys[0][t], ys[1][t]
        own_up.append(jnp.where(is_odd, o, e))
        own_down.append(jnp.where(is_odd, e, o))

    def group(tiles, slot, dst):
        return roll(tiles[slot // per], (dst - slot % per) * planes, 0)

    first = row < planes
    n = len(UP[1])
    for v in range(NV):
        c = VEL[v][1] if v < NQ else 0
        if c > 0:
            p = UP[1].index(v)
            edge = jnp.where(first, group(got_low, p, 0), group(own_up, n + p, 1))
        elif c < 0:
            p = DN[1].index(v)
            edge = jnp.where(first, group(own_down, n + p, 0), group(got_high, p, 1))
        else:
            p = 2 * n + (LV[1].index(v) if v < NQ else len(LV[1]) + v - NQ)
            edge = jnp.where(first, group(got_low, p, 0), group(got_high, p, 1))
        moved[v, planes] = edge
        for x in range(planes):
            q = value(v, x - 1)
            if c > 0:
                s = n + UP[1].index(v)
                line = roll(got_low[s // per], -((s % per) * planes + x), 0)
                q = jnp.where(row == 0, line, roll(q, 1, 0))
            elif c < 0:
                s = n + DN[1].index(v)
                line = roll(got_high[s // per], ly - 1 - ((s % per) * planes + x), 0)
                q = jnp.where(row == ly - 1, line, roll(q, -1, 0))
            moved[v, x] = q

    small = (ly, LANES)
    lane = iota(small, 1)
    up = jnp.zeros(small, jnp.float32)
    down = jnp.zeros(small, jnp.float32)
    for t in range(planes + 1):
        for p, (u, d) in enumerate(zip(UP[2], DN[2])):
            at = NV * t + 2 * p
            here = (lane == at) | (lane == at + 1)
            up = jnp.where(here, roll(moved[u, t, :, lz - LANES :], at + 2, 1), up)
            down = jnp.where(here, roll(moved[d, t, :, :LANES], at, 1), down)
        for q, v in enumerate(LV[2] + AUX):
            at = NV * t + 2 * len(UP[2]) + q
            here = lane == at
            up = jnp.where(here, roll(moved[v, t, :, lz - LANES :], at + 1, 1), up)
            down = jnp.where(here, roll(moved[v, t, :, :LANES], at, 1), down)
    is_odd = odd_mask("gz", small)
    ze[...] = jnp.where(is_odd, down, up)
    if two_z:
        zo[...] = jnp.where(is_odd, up, down)


def last_move(get, shifted, line):
    plus, minus = get(1, 0, 0), get(-1, 0, 0)
    density = get(0, 0, 0) + (plus + minus)
    mx = plus - minus
    lp, lm = line[1, 0], line[-1, 0]
    line_sum, line_diff = line[0, 0] + (lp + lm), lp - lm
    ways = []
    for cy in (1, -1):
        plus, minus = get(1, cy, 0), get(-1, cy, 0)
        ways.append(shifted(get(0, cy, 0) + (plus + minus), cy, line_sum))
        mx = mx + shifted(plus - minus, cy, line_diff)
    density = density + (ways[0] + ways[1])
    my = ways[0] - ways[1]
    ways = []
    for cz in (1, -1):
        plus, minus = get(1, 0, cz), get(-1, 0, cz)
        a = shifted(get(0, 1, cz), 1, line[0, cz])
        b = shifted(get(0, -1, cz), -1, line[0, cz])
        ways.append(roll(get(0, 0, cz) + (plus + minus) + (a + b), cz, 1))
        mx = mx + roll(plus - minus, cz, 1)
        my = my + roll(a - b, cz, 1)
    return density + (ways[0] + ways[1]), mx, my, ways[0] - ways[1]


def final_moments(moved, lx):
    planes = lx + 2
    post = {}
    for t in range(planes + 1):
        f = [roll(moved(i, t), VEL[i][2], 1) for i in range(NQ)]
        site = Site(f, [moved(v, t) for v in AUX])
        if t == planes:
            row = iota(f[0].shape, 0)
            edge = site.edge_rows(f, row < planes)
        elif t == 0 or t == planes - 1:
            for i in UP[0] if t == 0 else DN[0]:
                post[i, t] = site.post(VEL[i], weight(i), f[i], f[OPP[i]])
        else:
            for i, p in enumerate(site.post_all(f)):
                post[i, t] = p
    ly = row.shape[0]
    line = {k: (e if k[0] == 0 else roll(e, k[0], 0)) for k, e in edge.items()}
    result = []
    for t in range(1, lx + 1):

        def get(cx, cy, cz):
            return post[IDX[cx, cy, cz], t - cx]

        def shifted(main, cy, line):
            at, base = (0, 0) if cy > 0 else (ly - 1, planes)
            return jnp.where(row == at, roll(line, at - (base + t), 0), roll(main, cy, 0))

        result.append(last_move(get, shifted, line))
    return result


CUT = 4
HIGH, LOW, START = CUT, CUT + 2, CUT + 4


def inner_kernel(moved, inner, seam):
    planes = moved.shape[1] - 1
    ly, lz = moved.shape[2:]
    lane = iota((ly, LANES), 1)
    for v in range(NV):
        total = jnp.zeros((ly, LANES), jnp.float32)
        for t in range(planes + 1):
            at = NV * t
            last = roll(moved[v, t, :, lz - LANES :], at + CUT, 1)
            start = roll(moved[v, t, :, :LANES], at + START, 1)
            total = jnp.where((lane >= at) & (lane < at + CUT), last, total)
            total = jnp.where((lane >= at + START) & (lane < at + START + CUT), start, total)
        seam[v] = total
    for x, parts in enumerate(final_moments(lambda v, t: moved[v, t], planes - 2)):
        for a, p in enumerate(parts):
            inner[a, x] = p


def rim_kernel(nz, two_z, inner, seam, *refs):
    refs = list(refs)
    re = refs.pop(0)
    ro = refs.pop(0) if two_z else None
    density, momentum = refs
    lx, ly, lz = density.shape
    planes = lx + 2
    small = (ly, LANES)
    lane, row = iota(small, 1), iota(small, 0)
    low, high = halves("gz", nz, small)(re[...], None if ro is None else ro[...])

    def lanes_of(*places):
        mask = None
        for t in range(planes + 1):
            for p in places:
                here = lane == NV * t + p
                mask = here if mask is None else mask | here
        return mask

    two_low, two_high = lanes_of(LOW, LOW + 1), lanes_of(HIGH, HIGH + 1)
    one_low, one_high = lanes_of(LOW + 1), lanes_of(HIGH)

    def value(v):
        x = seam[v]
        c = VEL[v][2] if v < NQ else 0
        if c > 0:
            return jnp.where(two_low, roll(low, LOW - 2 * UP[2].index(v), 1), x)
        if c < 0:
            return jnp.where(two_high, roll(high, HIGH - 2 * DN[2].index(v), 1), x)
        at = 2 * len(UP[2]) + (LV[2].index(v) if v < NQ else len(LV[2]) + v - NQ)
        x = jnp.where(one_low, roll(low, LOW + 1 - at, 1), x)
        return jnp.where(one_high, roll(high, HIGH - at, 1), x)

    f = [roll(value(i), VEL[i][2], 1) for i in range(NQ)]
    site = Site(f, [value(v) for v in AUX])
    post = site.post_all(f)
    first = row < planes
    edge = site.edge_rows(f, first)
    near = {k: (e if k[0] == 0 else roll(e, k[0], 0)) for k, e in edge.items()}

    def get(cx, cy, cz):
        return roll(post[IDX[cx, cy, cz]], NV * cx, 1)

    def shifted(main, cy, line):
        at, base = (0, 0) if cy > 0 else (ly - 1, planes)
        out = roll(main, cy, 0)
        for t in range(1, lx + 1):
            part = roll(roll(line, NV * (t - planes), 1), at - (base + t), 0)
            out = jnp.where((row == at) & (lane >= NV * t) & (lane < NV * (t + 1)), part, out)
        return out

    total = last_move(get, shifted, near)
    for x in range(lx):
        for a in range(4):
            at = NV * (x + 1)
            parts = [inner[a, x, :, k : k + LANES] for k in range(0, lz, LANES)]
            parts[0] = jnp.where(lane < 2, roll(total[a], -(at + START), 1), parts[0])
            parts[-1] = jnp.where(lane >= LANES - 2, roll(total[a], -(at + CUT), 1), parts[-1])
            for k, p in enumerate(parts):
                if a == 0:
                    density[x, :, k * LANES : (k + 1) * LANES] = p
                else:
                    momentum[a - 1, x, :, k * LANES : (k + 1) * LANES] = p


def pair_routes(sizes):
    def linear(c):
        return (c[0] * sizes[1] + c[1]) * sizes[2] + c[2]

    routes = []
    for axis in range(3):
        own = []
        for odd in range(2 if sizes[axis] > 2 else 1):
            spare = [a for a in (1, 2, 0) if a != axis and sizes[a] % 2 == 0]
            route = []
            for c in np.ndindex(*sizes):
                other = list(c)
                k = ((c[axis] - odd) ^ 1) + odd
                if 0 <= k < sizes[axis]:
                    other[axis] = k
                elif spare:
                    other[spare[0]] ^= 1
                else:
                    continue
                route.append((linear(c), linear(other)))
            own.append(route)
        routes.append(own)
    return routes


def swap(messages, routes):
    return [lax.ppermute(m, AXES, r) for m, r in zip(messages, routes)]


VMEM = pl.BlockSpec(memory_space=pltpu.VMEM)
HBM = pl.BlockSpec(memory_space=pltpu.HBM)


def call(body, outs, flops, *args, specs=None, scratch=()):
    size = sum(int(np.prod(a.shape)) * 4 for a in args) + sum(int(np.prod(s)) * 4 for s in outs)
    return pl.pallas_call(
        body,
        out_shape=[jax.ShapeDtypeStruct(s, jnp.float32) for s in outs],
        in_specs=specs or [VMEM] * len(args),
        out_specs=[VMEM] * len(outs),
        scratch_shapes=scratch,
        cost_estimate=pl.CostEstimate(flops=flops, bytes_accessed=size, transcendentals=0),
        compiler_params=pltpu.CompilerParams(vmem_limit_bytes=16 << 20),
    )(*args)


def shards(sizes, dist, site_kinds, relax, inflow):
    lx, ly, lz = dist.shape[1:]
    planes = lx + 2
    assert ly == 2 * planes and lz % LANES == 0 and lz > LANES
    routes = pair_routes(sizes)
    two = [len(r) == 2 for r in routes]
    block = lx * ly * lz
    bulk, edge, ys = (NV, ly, lz), (-(-len(edge_rows(0, lx)) // ly), ly, lz), (NV * planes // ly, ly, lz)
    post, aux, *xm = call(
        functools.partial(first_kernel, two[0]),
        [dist.shape, (NA,) + site_kinds.shape] + [edge] * len(routes[0]) + [bulk] * len(routes[0]),
        250 * block,
        *[pltpu.with_memory_space_constraint(a, pltpu.HBM) for a in (dist, site_kinds, relax, inflow)],
        specs=[HBM] * 4,
        scratch=[
            pltpu.VMEM(dist.shape, jnp.float32),
            pltpu.VMEM(site_kinds.shape, jnp.int32),
            pltpu.SemaphoreType.DMA((4,)),
        ],
    )
    n = len(routes[0])
    xr = swap(xm[:n], routes[0])
    br = swap(xm[n:], routes[0])
    ym = call(
        functools.partial(second_kernel, sizes[0], two[0]),
        [ys, ys],
        100 * block,
        post, aux, *xr,
    )
    yr = swap(ym, routes[1])
    moved, *zm = call(
        functools.partial(third_kernel, sizes[0], sizes[1], two[0], two[1], two[2]),
        [(NV, planes + 1, ly, lz)] + [(ly, LANES)] * len(routes[2]),
        100 * block,
        post, aux, *br, *ym, *yr,
    )
    zr = swap(zm, routes[2])
    inner, seam = call(inner_kernel, [(4, lx, ly, lz), (NV, ly, LANES)], 300 * block, moved)
    density, momentum = call(
        functools.partial(rim_kernel, sizes[2], two[2]),
        [(lx, ly, lz), (3, lx, ly, lz)],
        100 * block,
        inner, seam, *zr,
    )
    return density, momentum


def solution(mesh):
    sizes = tuple(mesh.shape[a] for a in AXES)

    def body(*args):
        return shards(sizes, *args)

    return jax.shard_map(
        body,
        mesh=mesh,
        in_specs=(
            P(None, "gx", "gy", "gz"),
            P("gx", "gy", "gz"),
            P("gx", "gy", "gz"),
            P(None, "gx", "gy", "gz"),
        ),
        out_specs=(P("gx", "gy", "gz"), P(None, "gx", "gy", "gz")),
        check_vma=False,
    )
```

time: 30.8 us -> 21.1 us (0.69)
  Pallas kernels: 11.1 us -> 3.29 us
  starting transfers between devices: 6.43 us -> 9.84 us
  waiting for transfers between devices: 10.4 us -> 7.06 us
  local copies, waits for them, and re-layouts: 1.96 us -> 0 us
    pallas_call x4 -> x5, Pallas kernels: 11.1 us -> 3.29 us  [call(): pl.pallas_call(body, out_shape=[jax.ShapeDtypeStruct(s, jnp.float32) for...]
    ppermute x5 -> x7, starting transfers between devices: 6.43 us -> 9.84 us  [swap(): return [lax.ppermute(m, AXES, r) for m, r in zip(messages, routes)]]
    ppermute x5 -> x7, waiting for transfers between devices: 10.4 us -> 7.06 us  [swap(): return [lax.ppermute(m, AXES, r) for m, r in zip(messages, routes)]]
    unnamed x10 -> x0, local copies, waits for them, and re-layouts: 1.96 us -> none
  transfers between devices with their start and end apart: 5 -> 7, of which waited for: 3 -> 3; matrix products, arithmetic and copies ran while one was open for 0% -> 0% of each run, Pallas kernels for 0% -> 3%
where the time goes in v2:
time: 21.1 us; the launch traced here: 20.9 us
  starting transfers between devices  9.84 us (47%)
  waiting for transfers between devices  7.06 us (33%)
  Pallas kernels  3.29 us (16%)
  between operations  0.67 us (3%)
    ppermute x7, starting transfers between devices, swap(): return [lax.ppermute(m, AXES, r) for m, r in zip(messages, routes)]  9.84 us
    ppermute x7, waiting for transfers between devices, swap(): return [lax.ppermute(m, AXES, r) for m, r in zip(messages, routes)]  7.06 us
    pallas_call x5, Pallas kernels, call(): pl.pallas_call(body, out_shape=[jax.ShapeDtypeStruct(s, jnp.float32) for...  3.29 us
  transfers between devices with their start and end apart: 7, of which 3 were waited for; matrix products, arithmetic and copies ran while one was open for 0% of the time, Pallas kernels for 3%

profile of v2, /device:TPU:0, one launch (start us, length us, event | category | flops | bytes accessed | tf_op | source)
XLA Modules:
  0.0 20.9 jit_solution(17842225686055015263)
XLA Ops:
  0.6 1.3 %shard_map.59 = (f32[19,2,8,256]{3,2,1,0:T(8,128)S(1)}, f32[5,2,8,256]{3,2,1,0:T(8,128)S(1)}, f32[6,8,256]{2,1,0:T(8,128)S(1)}, f32[6,8,256]{2,1,0:T(8,128)S(1)}...) custom-call(f32[19,2,8,256]{3,2,1,0:T(8,128)} %dist.1, s32[2,8,256]{2,1,0:T(8,128)} %kinds.1, f32[2,8,256]{2,1,0:T(8,128)} %relax.1, ...), custom_call_target="tpu_custom_call" | custom-call | flops 1024000 | bytes 1277952 | tf_op jit(solution)/shard_map/pallas_call | solution.py:545
  1.9 3.1 %collective-permute-start = (f32[24,8,256]{2,1,0:T(8,128)S(1)}, f32[24,8,256]{2,1,0:T(8,128)S(1)}, u32[]{:S(2)}, u32[]{:S(2)}) collective-permute-start(f32[24,8,256]{2,1,0:T(8,128)S(1)} %get-tuple-element.16), channel_id=1, source_target_pairs={{0,8},{1,9},{2,10},{3,11},{4,12},{5,13},{6,14},{7,15},{8,0},{9,1},... | collective-permute-start | bytes 589832 | tf_op jit(solution)/shard_map/ppermute | solution.py:536
  5.0 0.0 collective-permute-start.1
  5.0 3.1 %collective-permute-start.2 = (f32[6,8,256]{2,1,0:T(8,128)S(1)}, f32[6,8,256]{2,1,0:T(8,128)S(1)}, u32[]{:S(2)}, u32[]{:S(2)}) collective-permute-start(f32[6,8,256]{2,1,0:T(8,128)S(1)} %get-tuple-element.18), channel_id=1, source_target_pairs={{0,8},{1,9},{2,10},{3,11},{4,12},{5,13},{6,14},{7,15},{8,0},{9,1},... | collective-permute-start | bytes 147464 | tf_op jit(solution)/shard_map/ppermute | solution.py:536
  8.2 0.0 collective-permute-start.3
  8.2 2.8 %collective-permute-done.2.refs_0_ = f32[6,8,256]{2,1,0:T(8,128)S(1)} collective-permute-done((f32[6,8,256]{2,1,0:T(8,128)S(1)}, f32[6,8,256]{2,1,0:T(8,128)S(1)}, u32[]{:S(2)}, u32[]{:S(2)}) %collective-permute-start.2) | collective-permute-done | bytes 49184 | tf_op jit(solution)/shard_map/ppermute | solution.py:536
  11.0 0.0 collective-permute-done.3.refs_1_
  11.0 0.1 shard_map.60
  11.1 0.1 collective-permute-start.4
  11.2 1.7 %collective-permute-start.5 = (f32[12,8,256]{2,1,0:T(8,128)S(1)}, f32[12,8,256]{2,1,0:T(8,128)S(1)}, u32[]{:S(2)}, u32[]{:S(2)}) collective-permute-start(f32[12,8,256]{2,1,0:T(8,128)S(1)} %get-tuple-element.21.refs_3_), channel_id=1, source_target_pairs={{0,1},{1,0},{2,4},{3,5},{4,2},{5,3},{6,7},{7,6},{8,9},{9,8},{10,12... | collective-permute-start | bytes 294920 | tf_op jit(solution)/shard_map/ppermute | solution.py:536
  12.9 0.0 collective-permute-done.4.refs_4_
  12.9 2.9 %collective-permute-done.5.refs_5_ = f32[12,8,256]{2,1,0:T(8,128)S(1)} collective-permute-done((f32[12,8,256]{2,1,0:T(8,128)S(1)}, f32[12,8,256]{2,1,0:T(8,128)S(1)}, u32[]{:S(2)}, u32[]{:S(2)}) %collective-permute-start.5) | collective-permute-done | bytes 98336 | tf_op jit(solution)/shard_map/ppermute | solution.py:536
  15.9 0.0 collective-permute-done.refs_0_
  15.9 0.0 collective-permute-done.1.refs_1_
  15.9 0.3 %shard_map.61 = (f32[24,5,8,256]{3,2,1,0:T(8,128)S(1)}, f32[8,128]{1,0:T(8,128)S(1)}) custom-call(f32[19,2,8,256]{3,2,1,0:T(8,128)S(1)} %get-tuple-element.14.post, f32[5,2,8,256]{3,2,1,0:T(8,128)S(1)} %get-tuple-element.15.aux, f32[24,8,256]{2,1,0:T(8,128)S(1)} %collective-permute-done.refs_0_, f32[24,8,256]{2,1,0:T(8,128)S(1)} %collective-permute-done.1.refs_1_, ...), custom_call_target="tpu_custom_call" | custom-call | flops 409600 | bytes 2166784 | tf_op jit(solution)/shard_map/pallas_call | solution.py:545
  16.2 1.7 %collective-permute-start.6 = (f32[8,128]{1,0:T(8,128)S(1)}, f32[8,128]{1,0:T(8,128)S(1)}, u32[]{:S(2)}, u32[]{:S(2)}) collective-permute-start(f32[8,128]{1,0:T(8,128)S(1)} %get-tuple-element.25), channel_id=1, source_target_pairs={{0,1},{1,0},{2,3},{3,2},{4,5},{5,4},{6,7},{7,6},{8,9},{9,8},{10,11... | collective-permute-start | bytes 12296 | tf_op jit(solution)/shard_map/ppermute | solution.py:536
  17.9 0.6 %shard_map.62 = (f32[4,2,8,256]{3,2,1,0:T(8,128)S(1)}, f32[24,8,128]{2,1,0:T(8,128)S(1)}) custom-call(f32[24,5,8,256]{3,2,1,0:T(8,128)S(1)} %get-tuple-element.22.moved), custom_call_target="tpu_custom_call" | custom-call | flops 1228800 | bytes 1146880 | tf_op jit(solution)/shard_map/pallas_call | solution.py:545
  18.5 1.3 %collective-permute-done.6.refs_0_ = f32[8,128]{1,0:T(8,128)S(1)} collective-permute-done((f32[8,128]{1,0:T(8,128)S(1)}, f32[8,128]{1,0:T(8,128)S(1)}, u32[]{:S(2)}, u32[]{:S(2)}) %collective-permute-start.6) | collective-permute-done | bytes 4128 | tf_op jit(solution)/shard_map/ppermute | solution.py:536
  19.8 1.0 %shard_map.63 = (f32[2,8,256]{2,1,0:T(8,128)}, f32[3,2,8,256]{3,2,1,0:T(8,128)}) custom-call(f32[4,2,8,256]{3,2,1,0:T(8,128)S(1)} %get-tuple-element.23.inner, f32[24,8,128]{2,1,0:T(8,128)S(1)} %get-tuple-element.24.seam, f32[8,128]{1,0:T(8,128)S(1)} %collective-permute-done.6.refs_0_), custom_call_target="tpu_custom_call" | custom-call | flops 409600 | bytes 233472 | tf_op jit(solution)/shard_map/pallas_call | solution.py:545
Async XLA Ops:
  1.9 14.0 %collective-permute-start = (f32[24,8,256]{2,1,0:T(8,128)S(1)}, f32[24,8,256]{2,1,0:T(8,128)S(1)}, u32[]{:S(2)}, u32[]{:S(2)}) collective-permute-start(f32[24,8,256]{2,1,0:T(8,128)S(1)} %get-tuple-element.16), channel_id=1, source_target_pairs={{0,8},{1,9},{2,10},{3,11},{4,12},{5,13},{6,14},{7,15},{8,0},{9,1},... | collective-permute-start | bytes 589832 | tf_op jit(solution)/shard_map/ppermute | solution.py:536
  5.0 10.8 %collective-permute-start.1 = (f32[24,8,256]{2,1,0:T(8,128)S(1)}, f32[24,8,256]{2,1,0:T(8,128)S(1)}, u32[]{:S(2)}, u32[]{:S(2)}) collective-permute-start(f32[24,8,256]{2,1,0:T(8,128)S(1)} %get-tuple-element.17), channel_id=1, source_target_pairs={{0,2},{1,3},{2,0},{3,1},{4,6},{5,7},{6,4},{7,5},{8,16},{9,17},{10,... | collective-permute-start | bytes 589832 | tf_op jit(solution)/shard_map/ppermute | solution.py:536
  5.0 6.0 %collective-permute-start.2 = (f32[6,8,256]{2,1,0:T(8,128)S(1)}, f32[6,8,256]{2,1,0:T(8,128)S(1)}, u32[]{:S(2)}, u32[]{:S(2)}) collective-permute-start(f32[6,8,256]{2,1,0:T(8,128)S(1)} %get-tuple-element.18), channel_id=1, source_target_pairs={{0,8},{1,9},{2,10},{3,11},{4,12},{5,13},{6,14},{7,15},{8,0},{9,1},... | collective-permute-start | bytes 147464 | tf_op jit(solution)/shard_map/ppermute | solution.py:536
  8.2 2.8 %collective-permute-start.3 = (f32[6,8,256]{2,1,0:T(8,128)S(1)}, f32[6,8,256]{2,1,0:T(8,128)S(1)}, u32[]{:S(2)}, u32[]{:S(2)}) collective-permute-start(f32[6,8,256]{2,1,0:T(8,128)S(1)} %get-tuple-element.19), channel_id=1, source_target_pairs={{0,2},{1,3},{2,0},{3,1},{4,6},{5,7},{6,4},{7,5},{8,16},{9,17},{10,... | collective-permute-start | bytes 147464 | tf_op jit(solution)/shard_map/ppermute | solution.py:536
  11.1 1.8 %collective-permute-start.4 = (f32[12,8,256]{2,1,0:T(8,128)S(1)}, f32[12,8,256]{2,1,0:T(8,128)S(1)}, u32[]{:S(2)}, u32[]{:S(2)}) collective-permute-start(f32[12,8,256]{2,1,0:T(8,128)S(1)} %get-tuple-element.20.refs_2_), channel_id=1, source_target_pairs={{0,2},{1,3},{2,0},{3,1},{4,6},{5,7},{6,4},{7,5},{8,10},{9,11},{10,... | collective-permute-start | bytes 294920 | tf_op jit(solution)/shard_map/ppermute | solution.py:536
  11.2 4.7 %collective-permute-start.5 = (f32[12,8,256]{2,1,0:T(8,128)S(1)}, f32[12,8,256]{2,1,0:T(8,128)S(1)}, u32[]{:S(2)}, u32[]{:S(2)}) collective-permute-start(f32[12,8,256]{2,1,0:T(8,128)S(1)} %get-tuple-element.21.refs_3_), channel_id=1, source_target_pairs={{0,1},{1,0},{2,4},{3,5},{4,2},{5,3},{6,7},{7,6},{8,9},{9,8},{10,12... | collective-permute-start | bytes 294920 | tf_op jit(solution)/shard_map/ppermute | solution.py:536
  16.2 3.7 %collective-permute-start.6 = (f32[8,128]{1,0:T(8,128)S(1)}, f32[8,128]{1,0:T(8,128)S(1)}, u32[]{:S(2)}, u32[]{:S(2)}) collective-permute-start(f32[8,128]{1,0:T(8,128)S(1)} %get-tuple-element.25), channel_id=1, source_target_pairs={{0,1},{1,0},{2,3},{3,2},{4,5},{5,4},{6,7},{7,6},{8,9},{9,8},{10,11... | collective-permute-start | bytes 12296 | tf_op jit(solution)/shard_map/ppermute | solution.py:536
